TPU v7x, 32 devices: a whole 2x2x4 slice. The times are simulated.
32 devices in a mesh: dp: 16 (over z, x, core), mp: 2 (over y).
Axes of the slice: x: 2, y: 2, z: 4, core: 2. Of those that a mesh axis runs over, the one named last changes fastest.
Arguments:
- inputs: bfloat16 [2, 16384, 768], P(None, ('dp', 'mp')), may hold values from -6 to 6
- roi_features: bfloat16 [2, 16384, 768], P(None, ('dp', 'mp')), may hold values from -6 to 6
- cotangent: bfloat16 [2, 16384, 768], P(None, ('dp', 'mp')), may hold values from -6 to 6
- doc_lengths: int32 [2, 16, 8], P(None, 'dp'), may hold values from 0 to 1024, as said below
- live_mask: int32 [2, 16384], P(None, 'dp'), may hold values 0 or 1
- bucket_cells: int32 [2, 3, 16384], P(None, None, 'dp'), may hold values from 0 to 31
- gain_attn: float32 [768], replicated, may hold values from 0.4 to 1.6
- gain_ffn: float32 [768], replicated, may hold values from 0.4 to 1.6
- w_query: bfloat16 [768, 768], P(None, 'mp'), may hold values from -0.21875 to 0.21875
- w_key: bfloat16 [768, 768], P(None, 'mp'), may hold values from -0.21875 to 0.21875
- w_value: bfloat16 [768, 768], P(None, 'mp'), may hold values from -0.21875 to 0.21875
- w_out: bfloat16 [768, 768], P('mp'), may hold values from -0.875 to 0.875
- w_up: bfloat16 [768, 3072], P(None, 'mp'), may hold values from -0.21875 to 0.21875
- w_down: bfloat16 [3072, 768], P('mp'), may hold values from -0.15625 to 0.15625
- bias_tables: float32 [3, 32, 12], P(None, None, 'mp'), may hold values from -4 to 4
Outputs:
- outputs: float32 [2, 16384, 768], P(None, ('dp', 'mp'))
- grad_inputs: float32 [2, 16384, 768], P(None, ('dp', 'mp'))
- grad_gain_attn: float32 [768], replicated
- grad_gain_ffn: float32 [768], replicated
- grad_w_query: float32 [768, 768], P(None, 'mp')
- grad_w_key: float32 [768, 768], P(None, 'mp')
- grad_w_value: float32 [768, 768], P(None, 'mp')
- grad_w_out: float32 [768, 768], P('mp')
- grad_w_up: float32 [768, 3072], P(None, 'mp')
- grad_w_down: float32 [3072, 768], P('mp')
- grad_bias_tables: float32 [3, 32, 12], P(None, None, 'mp')
Inputs may be any that keep to these rules, and one draw needn't show every extreme that they name: `doc_lengths`: each pack's 8 lengths sum to at most 1024; unused slots are 0; in every draw some pack is one document of 1024 tokens.
All inputs are finite; a program needn't handle non-finite values. No bound on the sum of `live_mask` on one device may be relied on, other than what follows from the above.
Results may differ from a plain program's by a relative error of at most 0.018.
Values may be sent and summed in bfloat16 or wider, within the bound.
A program may use at most 256 MiB of HBM per device.

v0:
```python
from functools import partial

import jax
import jax.numpy as jnp
from jax import lax
from jax.sharding import PartitionSpec as P

HDIM = 64


epsilon = 1e-06
masked_score = -1000000000.0
highest = lax.Precision.HIGHEST


def rms_scale(rows):
    return lax.rsqrt(jnp.mean(rows * rows, axis=-1, keepdims=True) + epsilon)


def rms_back(grad_normed, rows, inverse, gain):
    normed = rows * inverse
    grad_inner = grad_normed * gain
    grad_rows = inverse * (
        grad_inner - normed * jnp.mean(grad_inner * normed, axis=-1, keepdims=True)
    )
    return (grad_rows, jnp.sum(grad_normed * normed, axis=0))


def split_select(left, hot_low):
    upper = left.astype(jnp.bfloat16)
    rest = left - upper.astype(jnp.float32)
    middle = rest.astype(jnp.bfloat16)
    lower = (rest - middle.astype(jnp.float32)).astype(jnp.bfloat16)
    total = jnp.einsum("hqc,kc->hqk", upper, hot_low, preferred_element_type=jnp.float32)
    total = total + jnp.einsum("hqc,kc->hqk", middle, hot_low, preferred_element_type=jnp.float32)
    return total + jnp.einsum("hqc,kc->hqk", lower, hot_low, preferred_element_type=jnp.float32)


def local(
    inputs,
    roi_features,
    cotangent,
    doc_lengths,
    live_mask,
    bucket_cells,
    gain_attn,
    gain_ffn,
    w_query,
    w_key,
    w_value,
    w_out,
    w_up,
    w_down,
    bias_tables,
):
    micro = inputs.shape[0]
    local_rows = inputs.shape[1]
    model_width = inputs.shape[2]
    pack_len = live_mask.shape[1]
    width_local = w_query.shape[1]
    head_dim = HDIM
    heads_local = width_local // head_dim
    ffn_local = w_up.shape[1]
    buckets = bias_tables.shape[1]
    half = buckets // 2
    block_rows = min(512, pack_len)
    blocks = pack_len // block_rows
    factor = head_dim ** (-0.5)
    smooth_act = partial(jax.nn.gelu, approximate=False)
    proj_weight = jnp.concatenate([w_query, w_key, w_value], axis=1)
    cell_ids = jnp.arange(buckets)
    rel_small = jnp.clip(cell_ids[None, :] - cell_ids[:, None], -half, half - 1) + half
    select = (rel_small[:, :, None] == cell_ids[None, None, :]).astype(jnp.float32)
    bias_mats = jnp.einsum("abn,tnh->htab", select, bias_tables, precision=highest)
    key_ids = jnp.arange(pack_len)
    block_starts = jnp.arange(blocks) * block_rows
    acc_proj = jnp.zeros((model_width, 3 * width_local), jnp.float32)
    acc_out = jnp.zeros((width_local, model_width), jnp.float32)
    acc_up = jnp.zeros((model_width, ffn_local), jnp.float32)
    acc_down = jnp.zeros((ffn_local, model_width), jnp.float32)
    acc_mats = jnp.zeros((3, heads_local, buckets, buckets), jnp.float32)
    acc_gain_attn = jnp.zeros((model_width,), jnp.float32)
    acc_gain_ffn = jnp.zeros((model_width,), jnp.float32)
    out_list = []
    grad_list = []
    for batch_index in range(micro):
        lengths = doc_lengths[batch_index, 0]
        ends = jnp.cumsum(lengths)
        segment = jnp.sum((key_ids[:, None] >= ends[None, :]).astype(jnp.int32), axis=1)
        live = live_mask[batch_index]
        cells = bucket_cells[batch_index]
        one_hot = (cells.T[:, :, None] == cell_ids[None, None, :]).astype(jnp.float32)
        key_hot = one_hot.reshape(pack_len, 3 * buckets)
        key_hot_low = key_hot.astype(jnp.bfloat16)
        resid = inputs[batch_index].astype(jnp.float32) + roi_features[batch_index].astype(
            jnp.float32
        )
        inv_attn = rms_scale(resid)
        normed_attn = (resid * inv_attn * gain_attn).astype(jnp.bfloat16)
        piece = lax.all_gather(normed_attn, "mp", axis=0, tiled=True)
        made = jnp.dot(piece, proj_weight, preferred_element_type=jnp.float32).astype(jnp.bfloat16)
        joined = jnp.concatenate([piece, made], axis=1)
        full_normed = joined[:, :model_width]
        queries = joined[:, model_width : model_width + width_local].reshape(
            pack_len, heads_local, head_dim
        )
        keys_all = joined[:, model_width + width_local : model_width + 2 * width_local].reshape(
            pack_len, heads_local, head_dim
        )
        values_all = joined[:, model_width + 2 * width_local :].reshape(
            pack_len, heads_local, head_dim
        )
        query_blocks = queries.reshape(blocks, block_rows, heads_local, head_dim)
        seg_blocks = segment.reshape(blocks, block_rows)
        hot_blocks = one_hot.reshape(blocks, block_rows, 3, buckets)

        def block_scores(query_block, seg_block, hot_block, start):
            raw = (
                jnp.einsum(
                    "qhd,khd->hqk", query_block, keys_all, preferred_element_type=jnp.float32
                )
                * factor
            )
            left = jnp.einsum("qta,htab->hqtb", hot_block, bias_mats, precision=highest).reshape(
                heads_local, block_rows, 3 * buckets
            )
            bias = split_select(left, key_hot_low)
            row_ids = start + jnp.arange(block_rows)
            allowed = (seg_block[:, None] == segment[None, :]) & (
                (live[None, :] == 1) | (row_ids[:, None] == key_ids[None, :])
            )
            return jnp.where(allowed[None], raw + bias, masked_score)

        def attend(item):
            query_block, seg_block, hot_block, start = item
            scores = block_scores(query_block, seg_block, hot_block, start)
            top = jnp.max(scores, axis=-1, keepdims=True)
            expo = jnp.exp(scores - top)
            total = jnp.sum(expo, axis=-1, keepdims=True)
            probs = expo / total
            mixed = jnp.einsum(
                "hqk,khd->qhd",
                probs.astype(jnp.bfloat16),
                values_all,
                preferred_element_type=jnp.float32,
            ).astype(jnp.bfloat16)
            return (mixed.reshape(block_rows, width_local), (top + jnp.log(total))[..., 0])

        mixed_blocks, lse_blocks = lax.map(
            attend, (query_blocks, seg_blocks, hot_blocks, block_starts)
        )
        attn_mixed = mixed_blocks.reshape(pack_len, width_local)
        attn_added = lax.psum_scatter(
            jnp.dot(attn_mixed, w_out, preferred_element_type=jnp.float32),
            "mp",
            scatter_dimension=0,
            tiled=True,
        )
        hidden_res = resid + attn_added
        inv_ffn = rms_scale(hidden_res)
        normed_ffn = (hidden_res * inv_ffn * gain_ffn).astype(jnp.bfloat16)
        expand_piece = lax.all_gather(normed_ffn, "mp", axis=0, tiled=True)
        expand_made = smooth_act(
            jnp.dot(expand_piece, w_up, preferred_element_type=jnp.float32)
        ).astype(jnp.bfloat16)
        joined_ffn = jnp.concatenate([expand_piece, expand_made], axis=1)
        full_ffn_in = joined_ffn[:, :model_width]
        activ = joined_ffn[:, model_width:]
        ffn_added = lax.psum_scatter(
            jnp.dot(
                lax.slice_in_dim(activ, 0, local_rows * lax.axis_size("mp"), axis=0),
                w_down,
                preferred_element_type=jnp.float32,
            ).astype(jnp.bfloat16),
            "mp",
            scatter_dimension=0,
            tiled=True,
        ).astype(jnp.float32)
        out_list.append(hidden_res + ffn_added)
        grad_out_full = lax.all_gather(cotangent[batch_index], "mp", axis=0, tiled=True)
        acc_down = acc_down + jnp.einsum(
            "tf,td->fd", activ, grad_out_full, preferred_element_type=jnp.float32
        )
        grad_act = jnp.einsum(
            "td,fd->tf", grad_out_full, w_down, preferred_element_type=jnp.float32
        )
        pre_act = jnp.dot(full_ffn_in, w_up, preferred_element_type=jnp.float32)
        unused_value, act_pull = jax.vjp(smooth_act, pre_act)
        grad_pre = act_pull(grad_act)[0].astype(jnp.bfloat16)
        acc_up = acc_up + jnp.einsum(
            "td,tf->df", full_ffn_in, grad_pre, preferred_element_type=jnp.float32
        )
        grad_normed_ffn = lax.psum_scatter(
            jnp.einsum(
                "tf,df->td",
                lax.slice_in_dim(grad_pre, 0, local_rows * lax.axis_size("mp"), axis=0),
                w_up,
                preferred_element_type=jnp.float32,
            ),
            "mp",
            scatter_dimension=0,
            tiled=True,
        )
        grad_ffn_res, gain_part = rms_back(grad_normed_ffn, hidden_res, inv_ffn, gain_ffn)
        acc_gain_ffn = acc_gain_ffn + gain_part
        grad_hidden = cotangent[batch_index].astype(jnp.float32) + grad_ffn_res
        grad_hidden_full = lax.all_gather(
            grad_hidden.astype(jnp.bfloat16), "mp", axis=0, tiled=True
        )
        acc_out = acc_out + jnp.einsum(
            "tc,td->cd", attn_mixed, grad_hidden_full, preferred_element_type=jnp.float32
        )
        grad_mixed = jnp.einsum(
            "td,cd->tc", grad_hidden_full, w_out, preferred_element_type=jnp.float32
        ).astype(jnp.bfloat16)
        grad_blocks = grad_mixed.reshape(blocks, block_rows, heads_local, head_dim)

        def attend_back(carry, item):
            grad_keys, grad_values, grad_mats = carry
            query_block, seg_block, hot_block, start, grad_block, lse_block = item
            scores = block_scores(query_block, seg_block, hot_block, start)
            probs = jnp.exp(scores - lse_block[..., None])
            probs_low = probs.astype(jnp.bfloat16)
            grad_probs = jnp.einsum(
                "qhd,khd->hqk", grad_block, values_all, preferred_element_type=jnp.float32
            )
            row_dot = jnp.sum(grad_probs * probs, axis=-1, keepdims=True)
            grad_scores = (probs * (grad_probs - row_dot)).astype(jnp.bfloat16)
            grad_query = (
                jnp.einsum(
                    "hqk,khd->qhd", grad_scores, keys_all, preferred_element_type=jnp.float32
                )
                * factor
            ).astype(jnp.bfloat16)
            grad_keys = (
                grad_keys
                + jnp.einsum(
                    "hqk,qhd->khd", grad_scores, query_block, preferred_element_type=jnp.float32
                )
                * factor
            )
            grad_values = grad_values + jnp.einsum(
                "hqk,qhd->khd", probs_low, grad_block, preferred_element_type=jnp.float32
            )
            left = jnp.einsum(
                "hqk,kc->hqc", grad_scores, key_hot_low, preferred_element_type=jnp.float32
            ).reshape(heads_local, block_rows, 3, buckets)
            grad_mats = grad_mats + jnp.einsum("qta,hqtb->thab", hot_block, left, precision=highest)
            return (
                (grad_keys, grad_values, grad_mats),
                grad_query.reshape(block_rows, width_local),
            )

        zero_heads = jnp.zeros((pack_len, heads_local, head_dim), jnp.float32)
        zero_mats = jnp.zeros((3, heads_local, buckets, buckets), jnp.float32)
        back_carry, query_grads = lax.scan(
            attend_back,
            (zero_heads, zero_heads, zero_mats),
            (query_blocks, seg_blocks, hot_blocks, block_starts, grad_blocks, lse_blocks),
        )
        grad_keys, grad_values, grad_mats = back_carry
        acc_mats = acc_mats + grad_mats
        grad_proj = jnp.concatenate(
            [
                query_grads.reshape(pack_len, width_local),
                grad_keys.reshape(pack_len, width_local).astype(jnp.bfloat16),
                grad_values.reshape(pack_len, width_local).astype(jnp.bfloat16),
            ],
            axis=1,
        )
        acc_proj = acc_proj + jnp.einsum(
            "td,tc->dc", full_normed, grad_proj, preferred_element_type=jnp.float32
        )
        grad_normed_attn = lax.psum_scatter(
            jnp.einsum(
                "tc,dc->td", grad_proj, proj_weight, preferred_element_type=jnp.float32
            ).astype(jnp.bfloat16),
            "mp",
            scatter_dimension=0,
            tiled=True,
        ).astype(jnp.float32)
        grad_attn_res, gain_part = rms_back(grad_normed_attn, resid, inv_attn, gain_attn)
        acc_gain_attn = acc_gain_attn + gain_part
        grad_list.append(grad_hidden + grad_attn_res)
    table_grad = jnp.einsum("abn,thab->tnh", select, acc_mats, precision=highest)
    total_proj, total_out, total_up, total_down, total_table = lax.psum(
        (acc_proj, acc_out, acc_up, acc_down, table_grad), "dp"
    )
    gain_totals = lax.psum((acc_gain_attn, acc_gain_ffn), ("dp", "mp"))
    return (
        jnp.stack(out_list),
        jnp.stack(grad_list),
        gain_totals[0],
        gain_totals[1],
        total_proj[:, :width_local],
        total_proj[:, width_local : 2 * width_local],
        total_proj[:, 2 * width_local :],
        total_out,
        total_up,
        total_down,
        total_table,
    )


def solution(mesh):
    placed = (
        P(None, ("dp", "mp"), None),
        P(None, ("dp", "mp"), None),
        P(None, ("dp", "mp"), None),
        P(None, "dp", None),
        P(None, "dp"),
        P(None, None, "dp"),
        P(),
        P(),
        P(None, "mp"),
        P(None, "mp"),
        P(None, "mp"),
        P("mp", None),
        P(None, "mp"),
        P("mp", None),
        P(None, None, "mp"),
    )
    return jax.shard_map(
        local,
        mesh=mesh,
        in_specs=placed,
        out_specs=(
            P(None, ("dp", "mp"), None),
            P(None, ("dp", "mp"), None),
            P(),
            P(),
            P(None, "mp"),
            P(None, "mp"),
            P(None, "mp"),
            P("mp", None),
            P(None, "mp"),
            P("mp", None),
            P(None, None, "mp"),
        ),
        check_vma=False,
    )
```

profile of v0, /device:TPU:0, one launch (start us, length us, event | category | flops | bytes accessed | tf_op | source)
XLA Modules:
  0.0 1401.4 jit_solution(2280725634715378896)
XLA Ops:
  23.1 19.0 %all-gather.15.cloned.1.call-done = bf16[1024,768]{1,0:T(8,128)(2,1)} async-done(((bf16[512,768]{1,0:T(8,128)(2,1)}), bf16[1024,768]{1,0:T(8,128)(2,1)}) %all-gather.15.cloned.1.call-update) | async-done | bytes 1572880 | tf_op jit(solution)/shard_map/all_gather | solution.py:100
  56.9 14.4 %all-gather.11.cloned.1.call-done = bf16[1024,768]{1,0:T(8,128)(2,1)} async-done(((bf16[512,768]{1,0:T(8,128)(2,1)}), bf16[1024,768]{1,0:T(8,128)(2,1)}) %all-gather.11.cloned.1.call-update) | async-done | bytes 1572880 | tf_op jit(solution)/shard_map/all_gather | solution.py:100
  88.1 125.0 %while.60 = (s32[]{:T(128)}, bf16[2,512,384]{2,1,0:T(8,128)(2,1)}, f32[2,6,512]{2,1,0:T(8,128)S(1)}, s32[2,512]{1,0:T(2,128)S(1)}, s32[1024]{0:T(1024)S(1)}, /*i...) while((s32[]{:T(128)}, bf16[2,512,384]{2,1,0:T(8,128)(2,1)}, ...), condition=%wide.region_6.7_spmd.clone, body=%wide.region_3.6_spmd.clone.sunk | while | flops 2770041344 | bytes 183128720 | solution.py:149
  94.2 6.4 fusion.382
  100.6 6.4 fusion.383
  107.1 6.4 fusion.384
  113.5 20.4 %fusion.386 = (f32[6,512]{1,0:T(8,128)S(1)}, f32[6,512,1024]{2,1,0:T(8,128)}) fusion(bf16[6,512,96]{1,2,0:T(8,128)(2,1)} %get-tuple-element.1368, bf16[1024,96]{0,1:T(8,128)(2,1)} %copy-done.18, f32[6,512,1024]{2,1,0:T(8,128)} %fusion.382, f32[6,512,1024]{2,1,0:T(8,128)} %fusion.383, f32[6,512,1024]{2,1,0:T(8,128)} %fusion.384, ...), kind=kOutput, calls=%fused_computation.323.clone.1 | convolution fusion | flops 622851072 | bytes 51654656 | tf_op jit(solution)/shard_map/while/body/eval_jaxpr/hqc,kc->hqk/dot_general | solution.py:36
  133.9 7.6 fusion.387
  156.5 6.4 fusion.382
  162.9 6.4 fusion.383
  169.3 6.4 fusion.384
  175.7 20.4 %fusion.386 = (f32[6,512]{1,0:T(8,128)S(1)}, f32[6,512,1024]{2,1,0:T(8,128)}) fusion(bf16[6,512,96]{1,2,0:T(8,128)(2,1)} %get-tuple-element.1368, bf16[1024,96]{0,1:T(8,128)(2,1)} %copy-done.18, f32[6,512,1024]{2,1,0:T(8,128)} %fusion.382, f32[6,512,1024]{2,1,0:T(8,128)} %fusion.383, f32[6,512,1024]{2,1,0:T(8,128)} %fusion.384, ...), kind=kOutput, calls=%fused_computation.323.clone.1 | convolution fusion | flops 622851072 | bytes 51654656 | tf_op jit(solution)/shard_map/while/body/eval_jaxpr/hqc,kc->hqk/dot_general | solution.py:36
  196.1 7.6 fusion.387
  218.8 120.0 %while.61 = (s32[]{:T(128)}, bf16[2,512,384]{2,1,0:T(8,128)(2,1)}, f32[2,6,512]{2,1,0:T(8,128)S(1)}, s32[2,512]{1,0:T(2,128)S(1)}, s32[1024]{0:T(1024)S(1)}, /*i...) while((s32[]{:T(128)}, bf16[2,512,384]{2,1,0:T(8,128)(2,1)}, ...), condition=%wide.region_16.17_spmd.clone, body=%wide.region_13.16_spmd.clone.sunk | while | flops 2770041344 | bytes 189420240 | solution.py:149
  224.8 6.4 fusion.399
  231.2 6.4 fusion.400
  237.7 6.4 fusion.401
  244.1 20.5 %fusion.403 = (f32[6,512]{1,0:T(8,128)S(1)}, f32[6,512,1024]{2,1,0:T(8,128)}) fusion(bf16[6,512,96]{1,2,0:T(8,128)(2,1)} %get-tuple-element.1386, bf16[1024,96]{0,1:T(8,128)(2,1)} %copy-done.19, f32[6,512,1024]{2,1,0:T(8,128)} %fusion.399, f32[6,512,1024]{2,1,0:T(8,128)} %fusion.400, f32[6,512,1024]{2,1,0:T(8,128)} %fusion.401, ...), kind=kOutput, calls=%fused_computation.324.clone.1 | convolution fusion | flops 622851072 | bytes 51654656 | tf_op jit(solution)/shard_map/while/body/eval_jaxpr/hqc,kc->hqk/dot_general | solution.py:36
  264.6 7.6 fusion.404
  284.8 6.4 fusion.399
  291.2 6.4 fusion.400
  297.6 6.4 fusion.401
  304.1 20.4 %fusion.403 = (f32[6,512]{1,0:T(8,128)S(1)}, f32[6,512,1024]{2,1,0:T(8,128)}) fusion(bf16[6,512,96]{1,2,0:T(8,128)(2,1)} %get-tuple-element.1386, bf16[1024,96]{0,1:T(8,128)(2,1)} %copy-done.19, f32[6,512,1024]{2,1,0:T(8,128)} %fusion.399, f32[6,512,1024]{2,1,0:T(8,128)} %fusion.400, f32[6,512,1024]{2,1,0:T(8,128)} %fusion.401, ...), kind=kOutput, calls=%fused_computation.324.clone.1 | convolution fusion | flops 622851072 | bytes 51654656 | tf_op jit(solution)/shard_map/while/body/eval_jaxpr/hqc,kc->hqk/dot_general | solution.py:36
  324.4 7.6 fusion.404
  342.9 43.4 %reduce-scatter.13.cloned.1.call-done = f32[512,768]{1,0:T(8,128)} async-done(((f32[1024,768]{1,0:T(8,128)}), f32[512,768]{1,0:T(8,128)}) %reduce-scatter.13.cloned.1.call-update) | async-done | bytes 1572880 | tf_op jit(solution)/shard_map/reduce_scatter | solution.py:153
  395.9 24.6 %all-gather.13.cloned.1.call-done = bf16[1024,768]{1,0:T(8,128)(2,1)} async-done(((bf16[512,768]{1,0:T(8,128)(2,1)}), bf16[1024,768]{1,0:T(8,128)(2,1)}) %all-gather.13.cloned.1.call-update) | async-done | bytes 1572880 | tf_op jit(solution)/shard_map/all_gather | solution.py:162
  420.5 18.2 %multiply_convert_fusion.3 = (bf16[1024,1536]{1,0:T(8,128)(2,1)}, f32[1024,1536]{1,0:T(8,128)}, f32[1024,1536]{1,0:T(8,128)}) fusion(bf16[1024,768]{1,0:T(8,128)(2,1)} %all-gather.13.cloned.1.call-done, bf16[768,1536]{1,0:T(8,128)(2,1)S(1)} %copy-done), kind=kOutput, calls=%fused_computation.203 | convolution fusion | flops 2518155264 | bytes 19660800 | tf_op jit(solution)/shard_map/dot_general | solution.py:164
  438.8 11.0 all-gather.23.cloned.1.call-done
  449.7 9.8 add_convert_fusion.1
  465.6 43.4 %reduce-scatter.17.cloned.1.call-done = f32[512,768]{1,0:T(8,128)} async-done(((f32[1024,768]{1,0:T(8,128)}), f32[512,768]{1,0:T(8,128)}) %reduce-scatter.17.cloned.1.call-update) | async-done | bytes 1572880 | tf_op jit(solution)/shard_map/reduce_scatter | solution.py:193
  514.2 26.6 %all-gather.17.cloned.1.call-done = bf16[1024,768]{1,0:T(8,128)(2,1)} async-done(((bf16[512,768]{1,0:T(8,128)(2,1)}), bf16[1024,768]{1,0:T(8,128)(2,1)}) %all-gather.17.cloned.1.call-update) | async-done | bytes 1572880 | tf_op jit(solution)/shard_map/all_gather | solution.py:162
  540.8 18.6 %multiply_convert_fusion.2 = (bf16[1024,1536]{1,0:T(8,128)(2,1)}, f32[1024,1536]{1,0:T(8,128)}, f32[1024,1536]{1,0:T(8,128)}) fusion(bf16[1024,768]{1,0:T(8,128)(2,1)} %all-gather.17.cloned.1.call-done, bf16[768,1536]{1,0:T(8,128)(2,1)S(1)} %copy-done), kind=kOutput, calls=%fused_computation.190 | convolution fusion | flops 2518155264 | bytes 19660800 | tf_op jit(solution)/shard_map/dot_general | solution.py:164
  559.4 10.8 all-gather.25.cloned.1.call-done
  570.2 9.8 add_convert_fusion
  593.4 36.1 %reduce-scatter.21.cloned.1.call-done = f32[512,768]{1,0:T(8,128)} async-done(((f32[1024,768]{1,0:T(8,128)}), f32[512,768]{1,0:T(8,128)}) %reduce-scatter.21.cloned.1.call-update) | async-done | bytes 1572880 | tf_op jit(solution)/shard_map/reduce_scatter | solution.py:193
  632.5 25.4 %reduce-scatter.15.cloned.1.call-done = bf16[512,768]{1,0:T(8,128)(2,1)} async-done(((bf16[1024,768]{1,0:T(8,128)(2,1)}), bf16[512,768]{1,0:T(8,128)(2,1)}) %reduce-scatter.15.cloned.1.call-update) | async-done | bytes 786448 | tf_op jit(solution)/shard_map/reduce_scatter | solution.py:169
  663.5 26.5 %all-gather.21.cloned.1.call-done = bf16[1024,768]{1,0:T(8,128)(2,1)} async-done(((bf16[512,768]{1,0:T(8,128)(2,1)}), bf16[1024,768]{1,0:T(8,128)(2,1)}) %all-gather.21.cloned.1.call-update) | async-done | bytes 1572880 | tf_op jit(solution)/shard_map/all_gather | solution.py:207
  694.3 24.6 %all-gather.19.cloned.1.call-done = bf16[1024,768]{1,0:T(8,128)(2,1)} async-done(((bf16[512,768]{1,0:T(8,128)(2,1)}), bf16[1024,768]{1,0:T(8,128)(2,1)}) %all-gather.19.cloned.1.call-update) | async-done | bytes 1572880 | tf_op jit(solution)/shard_map/all_gather | solution.py:207
  724.1 155.1 %while.63 = (s32[]{:T(128)}, f32[1024,6,64]{0,2,1:T(8,128)}, f32[1024,6,64]{0,2,1:T(8,128)}, f32[3,6,32,32]{2,3,1,0:T(8,128)}, bf16[2,512,384]{2,1,0:T(8,128)(2,...) while((s32[]{:T(128)}, f32[1024,6,64]{0,2,1:T(8,128)}, ...), condition=%wide.region_31.32_spmd.clone, body=%wide.region_29.31_spmd.clone.sunk | while | flops 4700572160 | bytes 345035776 | solution.py:256
  729.6 6.4 fusion.456
  736.1 6.4 fusion.455
  742.5 6.4 fusion.457
  748.9 19.0 %subtract_exponential_fusion.7 = f32[6,512,1024]{2,1,0:T(8,128)} fusion(f32[6,512,1024]{2,1,0:T(8,128)} %fusion.455, f32[6,512,1024]{2,1,0:T(8,128)} %fusion.456, f32[6,512,1024]{2,1,0:T(8,128)} %fusion.457, f32[6,512]{1,0:T(8,128)S(1)} %dynamic-slice_bitcast_fusion.5, pred[512,1024]{1,0:T(8,128)(4,1)} %fusion.458, ...), kind=kOutput, calls=%fused_computation.131.clone.1 | convolution fusion | flops 622854144 | bytes 51654656 | tf_op jit(solution)/shard_map/while/body/eval_jaxpr/hqc,kc->hqk/dot_general | solution.py:36
  776.6 6.4 multiply_reduce_fusion.11
  807.1 6.4 fusion.456
  813.5 6.4 fusion.455
  819.9 6.4 fusion.457
  826.4 19.0 %subtract_exponential_fusion.7 = f32[6,512,1024]{2,1,0:T(8,128)} fusion(f32[6,512,1024]{2,1,0:T(8,128)} %fusion.455, f32[6,512,1024]{2,1,0:T(8,128)} %fusion.456, f32[6,512,1024]{2,1,0:T(8,128)} %fusion.457, f32[6,512]{1,0:T(8,128)S(1)} %dynamic-slice_bitcast_fusion.5, pred[512,1024]{1,0:T(8,128)(4,1)} %fusion.458, ...), kind=kOutput, calls=%fused_computation.131.clone.1 | convolution fusion | flops 622854144 | bytes 51654656 | tf_op jit(solution)/shard_map/while/body/eval_jaxpr/hqc,kc->hqk/dot_general | solution.py:36
  854.0 6.4 multiply_reduce_fusion.11
  888.2 167.5 %while.62 = (s32[]{:T(128)}, f32[1024,6,64]{0,2,1:T(8,128)}, f32[1024,6,64]{0,2,1:T(8,128)}, f32[3,6,32,32]{2,3,1,0:T(8,128)}, bf16[2,512,384]{2,1,0:T(8,128)(2,...) while((s32[]{:T(128)}, f32[1024,6,64]{0,2,1:T(8,128)}, ...), condition=%wide.region_24.25_spmd.clone, body=%wide.region_22.24_spmd.clone.sunk | while | flops 4700572160 | bytes 345035776 | solution.py:256
  905.9 6.4 fusion.428
  912.3 6.4 fusion.427
  918.7 6.4 fusion.429
  925.1 19.0 %subtract_exponential_fusion.6 = f32[6,512,1024]{2,1,0:T(8,128)} fusion(f32[6,512,1024]{2,1,0:T(8,128)} %fusion.427, f32[6,512,1024]{2,1,0:T(8,128)} %fusion.428, f32[6,512,1024]{2,1,0:T(8,128)} %fusion.429, f32[6,512]{1,0:T(8,128)S(1)} %dynamic-slice_bitcast_fusion.4, pred[512,1024]{1,0:T(8,128)(4,1)} %fusion.430, ...), kind=kOutput, calls=%fused_computation.76.clone.1 | convolution fusion | flops 622854144 | bytes 51654656 | tf_op jit(solution)/shard_map/while/body/eval_jaxpr/hqc,kc->hqk/dot_general | solution.py:36
  952.8 6.4 multiply_reduce_fusion.10
  983.2 6.4 fusion.428
  989.6 6.4 fusion.427
  996.0 6.4 fusion.429
  1002.5 19.0 %subtract_exponential_fusion.6 = f32[6,512,1024]{2,1,0:T(8,128)} fusion(f32[6,512,1024]{2,1,0:T(8,128)} %fusion.427, f32[6,512,1024]{2,1,0:T(8,128)} %fusion.428, f32[6,512,1024]{2,1,0:T(8,128)} %fusion.429, f32[6,512]{1,0:T(8,128)S(1)} %dynamic-slice_bitcast_fusion.4, pred[512,1024]{1,0:T(8,128)(4,1)} %fusion.430, ...), kind=kOutput, calls=%fused_computation.76.clone.1 | convolution fusion | flops 622854144 | bytes 51654656 | tf_op jit(solution)/shard_map/while/body/eval_jaxpr/hqc,kc->hqk/dot_general | solution.py:36
  1030.2 6.4 multiply_reduce_fusion.10
  1063.7 6.4 convolution_convert_fusion.5
  1101.7 63.4 %psum.55 = f32[3,32,6]{1,2,0:T(8,128)} all-reduce(f32[3,32,6]{1,2,0:T(8,128)S(1)} %convolution_bitcast_fusion.5), channel_id=1, replica_groups=mesh['dp'=16,'mp'=2] {'dp'}, use_global_device_ids=true, to_apply=%region_44.45 | all-reduce | flops 576 | bytes 4608 | tf_op jit(solution)/shard_map/psum | solution.py:286
  1168.6 39.1 %all-reduce = (f32[768]{0:T(1024)}, f32[768]{0:T(1024)}) all-reduce(f32[768]{0:T(1024)S(1)} %add.285, f32[768]{0:T(1024)S(1)} %add.286), channel_id=1, replica_groups=mesh['dp'=16,'mp'=2] {'dp','mp'}, use_global_device_ids=true, to_apply=%region_36.37 | all-reduce | flops 1536 | bytes 12288 | tf_op jit(solution)/shard_map/psum | solution.py:289
  1219.8 164.1 %all-reduce.4.cloned.1.call-done = (f32[768,1152]{1,0:T(8,128)}, f32[384,768]{1,0:T(8,128)}, f32[768,1536]{1,0:T(8,128)}, f32[1536,768]{1,0:T(8,128)}) async-done(((f32[768,1152]{1,0:T(8,128)}, f32[384,768]{1,0:T(8,128)}, f32[768,1536]{1,0:T(8,128)}, f32[1536,768]{1,0:T(8,128)}), (f32[768,1152]{1,0:T(8,128)}, f32[384,768]{1,0:T(8,128)}, f32[768,1536]{1,0:T(8,128)}, ...) | async-done | bytes 14155792 | tf_op jit(solution)/shard_map/psum | solution.py:286
  (591 shorter events, 368.2 us)
Async XLA Ops:
  7.2 413.4 %copy-start = (bf16[768,1536]{1,0:T(8,128)(2,1)S(1)}, bf16[768,1536]{1,0:T(8,128)(2,1)}, u32[]{:S(2)}) copy-start(bf16[768,1536]{1,0:T(8,128)(2,1)} %param.35) | copy-start | bytes 7077892
  7.2 34.8 %all-gather.15.cloned.1.call-start = ((), (), s32[]{:S(2)}) async-start(), calls=%async_computation.12 | async-start | bytes 2359296 | tf_op jit(solution)/shard_map/all_gather | solution.py:100
  11.9 59.4 %all-gather.11.cloned.1.call-start = ((), (), s32[]{:S(2)}) async-start(), calls=%async_computation.8 | async-start | bytes 2359296 | tf_op jit(solution)/shard_map/all_gather | solution.py:100
  12.7 330.2 %reduce-scatter.9.cloned.1.call-start = ((), (), s32[]{:S(2)}) async-start(), calls=%async_computation.9 | async-start | bytes 4718592 | tf_op jit(solution)/shard_map/reduce_scatter | solution.py:153
  12.8 33.4 %copy-start.82 = (s32[32,32]{1,0:T(8,128)}, s32[32,32]{1,0:T(8,128)S(1)}, u32[]{:S(2)}) copy-start(s32[32,32]{1,0:T(8,128)S(1)} %clamp_add_fusion) | copy-start | bytes 12292
  89.6 11.0 copy-start.18
  133.9 8.3 copy-start.8
  151.9 11.0 copy-start.18
  196.1 8.3 copy-start.8
  217.8 168.5 %reduce-scatter.13.cloned.1.call-start = ((), (), s32[]{:S(2)}) async-start(), calls=%async_computation.13 | async-start | bytes 4718592 | tf_op jit(solution)/shard_map/reduce_scatter | solution.py:153
  220.2 11.0 copy-start.19
  244.1 28.1 %copy-start.39 = (bf16[1024,6,64]{0,2,1:T(8,128)(2,1)S(1)}, bf16[1024,6,64]{0,2,1:T(8,128)(2,1)}, u32[]{:S(2)}) copy-start(bf16[1024,6,64]{0,2,1:T(8,128)(2,1)} %get-tuple-element.1520) | copy-start | bytes 2359300 | tf_op jit(solution)/shard_map/while
  264.6 8.3 copy-start.9
  280.2 11.0 copy-start.19
  304.1 28.0 %copy-start.39 = (bf16[1024,6,64]{0,2,1:T(8,128)(2,1)S(1)}, bf16[1024,6,64]{0,2,1:T(8,128)(2,1)}, u32[]{:S(2)}) copy-start(bf16[1024,6,64]{0,2,1:T(8,128)(2,1)} %get-tuple-element.1520) | copy-start | bytes 2359300 | tf_op jit(solution)/shard_map/while
  324.4 8.3 copy-start.9
  342.8 49.2 %copy-start.80 = (f32[768]{0:T(1024)S(1)}, f32[768]{0:T(1024)}, u32[]{:S(2)}) copy-start(f32[768]{0:T(1024)} %param.30) | copy-start | bytes 9220
  342.8 77.7 %all-gather.13.cloned.1.call-start = ((), (), s32[]{:S(2)}) async-start(), calls=%async_computation.10 | async-start | bytes 2359296 | tf_op jit(solution)/shard_map/all_gather | solution.py:162
  390.9 267.0 %copy-start.89 = (f32[512]{0:T(512)}, f32[512]{0:T(512)S(1)}, u32[]{:S(2)}) copy-start(f32[512]{0:T(512)S(1)} %add_rsqrt_fusion.2) | copy-start | bytes 6148
  393.2 56.6 %all-gather.23.cloned.1.call-start = ((), (), s32[]{:S(2)}) async-start(), calls=%async_computation.22 | async-start | bytes 2359296 | tf_op jit(solution)/shard_map/all_gather | solution.py:180
  395.8 113.2 %reduce-scatter.17.cloned.1.call-start = ((), (), s32[]{:S(2)}) async-start(), calls=%async_computation.16 | async-start | bytes 4718592 | tf_op jit(solution)/shard_map/reduce_scatter | solution.py:193
  465.5 75.3 %all-gather.17.cloned.1.call-start = ((), (), s32[]{:S(2)}) async-start(), calls=%async_computation.14 | async-start | bytes 2359296 | tf_op jit(solution)/shard_map/all_gather | solution.py:162
  465.6 192.3 %copy-start.91 = (f32[512]{0:T(512)}, f32[512]{0:T(512)S(1)}, u32[]{:S(2)}) copy-start(f32[512]{0:T(512)S(1)} %add_rsqrt_fusion) | copy-start | bytes 6148
  513.4 56.8 %all-gather.25.cloned.1.call-start = ((), (), s32[]{:S(2)}) async-start(), calls=%async_computation.23 | async-start | bytes 2359296 | tf_op jit(solution)/shard_map/all_gather | solution.py:180
  514.2 115.4 %reduce-scatter.21.cloned.1.call-start = ((), (), s32[]{:S(2)}) async-start(), calls=%async_computation.19 | async-start | bytes 4718592 | tf_op jit(solution)/shard_map/reduce_scatter | solution.py:193
  586.0 71.9 %reduce-scatter.15.cloned.1.call-start = ((), (), s32[]{:S(2)}) async-start(), calls=%async_computation.15 | async-start | bytes 2359296 | tf_op jit(solution)/shard_map/reduce_scatter | solution.py:169
  593.4 64.6 %copy-start.33 = (f32[512,768]{1,0:T(8,128)S(1)}, f32[512,768]{1,0:T(8,128)}, u32[]{:S(2)}) copy-start(f32[512,768]{1,0:T(8,128)} %copy-done.32) | copy-start | bytes 4718596
  593.4 96.6 %all-gather.21.cloned.1.call-start = ((), (), s32[]{:S(2)}) async-start(), calls=%async_computation.20 | async-start | bytes 2359296 | tf_op jit(solution)/shard_map/all_gather | solution.py:207
  593.4 69.1 %copy-start.98 = (f32[512]{0:T(512)}, f32[512]{0:T(512)S(1)}, u32[]{:S(2)}) copy-start(f32[512]{0:T(512)S(1)} %broadcast_multiply_fusion.3) | copy-start | bytes 6148
  632.5 30.1 %copy-start.100 = (f32[512]{0:T(512)}, f32[512]{0:T(512)S(1)}, u32[]{:S(2)}) copy-start(f32[512]{0:T(512)S(1)} %broadcast_multiply_fusion.1) | copy-start | bytes 6148
  632.5 57.5 %copy-start.57 = (bf16[384,768]{1,0:T(8,128)(2,1)S(1)}, bf16[384,768]{1,0:T(8,128)(2,1)}, u32[]{:S(2)}) copy-start(bf16[384,768]{1,0:T(8,128)(2,1)} %param.34) | copy-start | bytes 1769476
  662.6 56.2 %all-gather.19.cloned.1.call-start = ((), (), s32[]{:S(2)}) async-start(), calls=%async_computation.17 | async-start | bytes 2359296 | tf_op jit(solution)/shard_map/all_gather | solution.py:207
  663.4 501.8 %reduce-scatter.23.cloned.1.call-start = ((), (), s32[]{:S(2)}) async-start(), calls=%async_computation.21 | async-start | bytes 2359296 | tf_op jit(solution)/shard_map/reduce_scatter | solution.py:274
  748.9 19.0 %copy-start.29 = (f32[1024,6,64]{0,2,1:T(8,128)S(1)}, f32[1024,6,64]{0,2,1:T(8,128)}, u32[]{:S(2)}) copy-start(f32[1024,6,64]{0,2,1:T(8,128)} %get-tuple-element.1606) | copy-start | bytes 4718596 | tf_op jit(solution)/shard_map/while
  767.9 8.3 copy-start.2
  767.9 8.4 copy-start.40
  767.9 8.6 copy-start.42
  826.4 19.0 %copy-start.29 = (f32[1024,6,64]{0,2,1:T(8,128)S(1)}, f32[1024,6,64]{0,2,1:T(8,128)}, u32[]{:S(2)}) copy-start(f32[1024,6,64]{0,2,1:T(8,128)} %get-tuple-element.1606) | copy-start | bytes 4718596 | tf_op jit(solution)/shard_map/while
  845.4 8.3 copy-start.2
  845.4 8.4 copy-start.40
  845.4 8.6 copy-start.42
  881.7 6.5 copy-start.59
  881.7 6.5 copy-start.71
  881.7 6.5 copy-start.75
  881.8 6.5 copy-start.78
  887.2 278.0 %reduce-scatter.19.cloned.1.call-start = ((), (), s32[]{:S(2)}) async-start(), calls=%async_computation.18 | async-start | bytes 2359296 | tf_op jit(solution)/shard_map/reduce_scatter | solution.py:274
  925.1 19.0 %copy-start.26 = (f32[1024,6,64]{0,2,1:T(8,128)S(1)}, f32[1024,6,64]{0,2,1:T(8,128)}, u32[]{:S(2)}) copy-start(f32[1024,6,64]{0,2,1:T(8,128)} %get-tuple-element.1546) | copy-start | bytes 4718596 | tf_op jit(solution)/shard_map/while
  944.2 8.3 copy-start.3
  944.2 8.4 copy-start.38
  944.2 8.6 copy-start.41
  1002.5 19.0 %copy-start.26 = (f32[1024,6,64]{0,2,1:T(8,128)S(1)}, f32[1024,6,64]{0,2,1:T(8,128)}, u32[]{:S(2)}) copy-start(f32[1024,6,64]{0,2,1:T(8,128)} %get-tuple-element.1546) | copy-start | bytes 4718596 | tf_op jit(solution)/shard_map/while
  1021.5 8.3 copy-start.3
  1021.5 8.4 copy-start.38
  1021.5 8.6 copy-start.41
  1063.7 148.9 %reduce-scatter.11.cloned.1.call-start = ((), (), s32[]{:S(2)}) async-start(), calls=%async_computation.11 | async-start | bytes 2359296 | tf_op jit(solution)/shard_map/reduce_scatter | solution.py:169
  1070.1 313.8 %all-reduce.4.cloned.1.call-start = ((), (), s32[]{:S(2)}) async-start(), calls=%async_computation.24 | async-start | bytes 28311552 | tf_op jit(solution)/shard_map/psum | solution.py:286
  1099.7 65.5 %copy-start.36 = (bf16[2,512,768]{2,1,0:T(8,128)(2,1)S(1)}, bf16[2,512,768]{2,1,0:T(8,128)(2,1)}, u32[]{:S(2)}) copy-start(bf16[2,512,768]{2,1,0:T(8,128)(2,1)} %param.24) | copy-start | bytes 4718596
  1099.7 65.5 %copy-start.88 = (f32[768]{0:T(1024)S(1)}, f32[768]{0:T(1024)}, u32[]{:S(2)}) copy-start(f32[768]{0:T(1024)} %param.29) | copy-start | bytes 9220
  1099.7 65.5 %copy-start.94 = (f32[512]{0:T(512)S(1)}, f32[512]{0:T(512)}, u32[]{:S(2)}) copy-start(f32[512]{0:T(512)} %copy-done.93) | copy-start | bytes 6148
  1099.7 65.5 %copy-start.96 = (f32[512]{0:T(512)S(1)}, f32[512]{0:T(512)}, u32[]{:S(2)}) copy-start(f32[512]{0:T(512)} %copy-done.95) | copy-start | bytes 6148
  1100.8 106.9 %copy-start.81 = (f32[768]{0:T(1024)S(1)}, f32[768]{0:T(1024)}, u32[]{:S(2)}) copy-start(f32[768]{0:T(1024)} %param.30) | copy-start | bytes 9220
  1100.8 106.9 %copy-start.92 = (f32[512]{0:T(512)S(1)}, f32[512]{0:T(512)}, u32[]{:S(2)}) copy-start(f32[512]{0:T(512)} %copy-done.91) | copy-start | bytes 6148
  1100.8 106.9 %copy-start.101 = (f32[512]{0:T(512)S(1)}, f32[512]{0:T(512)}, u32[]{:S(2)}) copy-start(f32[512]{0:T(512)} %copy-done.100) | copy-start | bytes 6148
  1165.2 42.5 %copy-start.56 = (bf16[512,768]{1,0:T(8,128)(2,1)S(1)}, bf16[512,768]{1,0:T(8,128)(2,1)}, u32[]{:S(2)}) copy-start(bf16[512,768]{1,0:T(8,128)(2,1)} %reduce-scatter.23.cloned.1.call-done) | copy-start | bytes 2359300
  (109 other events, 412.8 us)
Sparse Core Ops, SparseCore 0:
  12.1 29.8 all-gather.14
  44.1 27.2 all-gather.10
  217.9 43.3 reduce-scatter.8
  342.9 43.3 reduce-scatter.12
  393.3 27.2 all-gather.12
  422.5 27.2 all-gather.22
  465.7 43.3 reduce-scatter.16
  513.5 27.2 all-gather.16
  543.0 27.2 all-gather.24
  586.2 43.3 reduce-scatter.20
  631.8 26.0 reduce-scatter.14
  662.7 27.2 all-gather.20
  691.6 27.1 all-gather.18
  887.3 26.0 reduce-scatter.22
  1063.8 26.0 reduce-scatter.18
  1092.1 26.0 reduce-scatter.10
  1123.8 260.0 all-reduce.3
where the time goes:
time: 1410 us; the launch traced here: 1400 us
  matrix products  577 us (41%)
  waiting for transfers between devices  472 us (33%)
  other arithmetic  118 us (8%)
  blocking collectives  103 us (7%)
  local copies, waits for them, and re-layouts  100 us (7%)
  between operations  15.3 us (1%)
  loops' own time  14.7 us (1%)
    psum x1, waiting for transfers between devices, local(): lax.psum((acc_proj, acc_out, acc_up, acc_down, table_grad), 'dp')  164 us
    dot_general x8, matrix products, split_select(): jnp.einsum('hqc,kc->hqk', lower, hot_low, preferred_element_type=jnp.floa...  158 us
    reduce_scatter x2, waiting for transfers between devices, local(): lax.psum_scatter(jnp.einsum('tf,df->td', lax.slice_in_dim(grad_pre, 0, lo...  79.5 us
    psum x1, blocking collectives, local(): lax.psum((acc_proj, acc_out, acc_up, acc_down, table_grad), 'dp')  63.4 us
    dot_general x8, matrix products, block_scores(): jnp.einsum('qhd,khd->hqk', query_block, keys_all, preferred_element_type=...  51.5 us
    dot_general x8, matrix products, split_select(): jnp.einsum('hqc,kc->hqk', middle, hot_low, preferred_element_type=jnp.flo...  51.3 us
    all_gather x2, waiting for transfers between devices, local(): expand_piece = lax.all_gather(normed_ffn, 'mp', axis=0, tiled=True)  51.2 us
    dot_general x8, matrix products, split_select(): jnp.einsum('hqc,kc->hqk', upper, hot_low, preferred_element_type=jnp.floa...  51.2 us
  transfers between devices with their start and end apart: 17, of which 13 were waited for; matrix products, arithmetic and copies ran while one was open for 29% of the time, Pallas kernels for 0%

commit v1 on v0

v1 whole, which is shorter than its diff:
```python
import functools
import math

import jax
import jax.numpy as jnp
from jax import lax
from jax.experimental import pallas as pl
from jax.experimental.pallas import tpu as pltpu
from jax.sharding import PartitionSpec as P

BF = jnp.bfloat16
F32 = jnp.float32
HDIM = 64
EPS = 1e-06
MASKED = -1e30
MESH = pl.DeviceIdType.MESH
VMEM = pl.BlockSpec(memory_space=pltpu.VMEM)
ANY = pl.BlockSpec(memory_space=pl.ANY)
SHAPE = jax.ShapeDtypeStruct


def dg(a, b, ca, cb):
    return lax.dot_general(a, b, (((ca,), (cb,)), ((), ())), preferred_element_type=F32)


def params(limit=58, **more):
    return pltpu.CompilerParams(vmem_limit_bytes=limit << 20, **more)


class Links:
    def __init__(self, send, recv):
        self.send, self.recv, self.count = send, recv, 0
        self.d, self.m = lax.axis_index("dp"), lax.axis_index("mp")

    def remote(self, src, dst, dp_flip=0, mp_flip=0):
        i = self.count
        self.count += 1
        dp = self.d ^ dp_flip if dp_flip else self.d
        mp = self.m ^ mp_flip if mp_flip else self.m
        return pltpu.make_async_remote_copy(
            src_ref=src,
            dst_ref=dst,
            send_sem=self.send.at[i],
            recv_sem=self.recv.at[i],
            device_id=(dp, mp),
            device_id_type=MESH,
        )

    def local(self, src, dst):
        i = self.count
        self.count += 1
        return pltpu.make_async_copy(src, dst, self.send.at[i])

    def barrier(self, flips):
        sem = pltpu.get_barrier_semaphore()
        for dp_flip, mp_flip in flips:
            dp = self.d ^ dp_flip if dp_flip else self.d
            mp = self.m ^ mp_flip if mp_flip else self.m
            pl.semaphore_signal(sem, inc=1, device_id=(dp, mp), device_id_type=MESH)
        pl.semaphore_wait(sem, len(flips))


def rows_at(start, size, unit):
    return pl.ds(pl.multiple_of(start, unit), size)


def gather_kernel(
    hi, cot, tab, wq, wk, wv, wo, wup, wdn,
    xf, dyf, tabo, qkvf, wof, wupf, wdnf,
    send, recv,
):
    links = Links(send, recv)
    d, m = links.d, links.m
    rows = hi.shape[1]
    width = wq.shape[0]
    third = wq.shape[1]
    hidden = wup.shape[1]
    inner = wo.shape[0]
    links.barrier(((0, 1), (1, 0), (2, 0), (4, 0)))
    core, cross, deep = d & 1, (d >> 1) & 1, (d >> 2) & 1
    other = 1 - m
    locals_ = []
    own_rows = rows_at(m * rows, rows, rows)
    waits = []

    def go(copy):
        copy.start()
        waits.append(copy)
        return copy

    targets = (
        (qkvf, 0, width, slice(3 * third, 6 * third)),
        (wof, inner, inner, slice(0, width)),
        (wupf, 0, width, slice(hidden, 2 * hidden)),
        (wdnf, hidden, hidden, slice(0, width)),
    )
    sources = ((wq, wk, wv), (wo,), (wup,), (wdn,))

    def block(entry, first, count):
        full, base, total, columns = entry
        piece = total // 8
        return full.at[rows_at(base + first * piece, count * piece, piece), columns]

    place = core * 4 + cross * 2 + deep
    stage_y = []
    for entry, parts in zip(targets, sources):
        full, base, total, columns = entry
        piece = total // 8
        group = []
        for j, part in enumerate(parts):
            span = part.shape[1]
            cols = slice(columns.start + j * span, columns.start + (j + 1) * span)
            group.append(
                go(
                    links.remote(
                        part.at[rows_at(place * piece, piece, piece)],
                        full.at[rows_at(base + place * piece, piece, piece), cols],
                        mp_flip=1,
                    )
                )
            )
        stage_y.append(group)
        if full is qkvf:
            row_copies = [
                go(links.remote(tab, tabo, mp_flip=1)),
                go(links.remote(hi.at[other], xf.at[own_rows], mp_flip=1)),
            ]
    row_copies.append(go(links.remote(cot.at[other], dyf.at[own_rows], mp_flip=1)))
    locals_.append(links.local(hi.at[m], xf.at[own_rows]))
    locals_.append(links.local(cot.at[m], dyf.at[own_rows]))
    for j, part in enumerate((wq, wk, wv)):
        locals_.append(links.local(part, qkvf.at[:, j * third : (j + 1) * third]))
    locals_.append(links.local(wo, wof.at[0:inner]))
    locals_.append(links.local(wup, wupf.at[:, 0:hidden]))
    locals_.append(links.local(wdn, wdnf.at[0:hidden]))
    for copy in locals_:
        copy.start()
    stage = stage_y
    for flip, first, count in (
        (4, place, 1),
        (2, core * 4 + cross * 2, 2),
        (1, core * 4, 4),
    ):
        following = []
        for entry, group in zip(targets, stage):
            for copy in group:
                copy.wait_recv()
            there = block(entry, first, count)
            following.append([go(links.remote(there, there, dp_flip=flip))])
        stage = following
    for group in stage:
        for copy in group:
            copy.wait_recv()
    for copy in row_copies:
        copy.wait_recv()
    for copy in waits:
        copy.wait_send()
    for copy in locals_:
        copy.wait()


def gather(hi, cot, tab, wq, wk, wv, wo, wup, wdn):
    rows, width = hi.shape[1], hi.shape[2]
    third, hidden = wq.shape[1], wup.shape[1]
    return pl.pallas_call(
        gather_kernel,
        out_shape=[
            SHAPE((2 * rows, width), BF),
            SHAPE((2 * rows, width), BF),
            SHAPE(tab.shape, F32),
            SHAPE((width, 6 * third), BF),
            SHAPE((2 * third, width), BF),
            SHAPE((width, 2 * hidden), BF),
            SHAPE((2 * hidden, width), BF),
        ],
        in_specs=[ANY] * 9,
        out_specs=[ANY] * 7,
        scratch_shapes=[pltpu.SemaphoreType.DMA((40,)), pltpu.SemaphoreType.DMA((40,))],
        compiler_params=params(16, collective_id=1, has_side_effects=True),
        name="gather",
    )(hi, cot, tab, wq, wk, wv, wo, wup, wdn)


def proj_kernel(x_ref, g_ref, w_ref, q_ref, kv_ref, *, third):
    x = x_ref[...].astype(F32)
    inverse = lax.rsqrt(jnp.mean(x * x, axis=-1, keepdims=True) + EPS)
    normed = (x * inverse * g_ref[...]).astype(BF)
    w = w_ref[...]
    q_ref[...] = dg(w[:, 0:third], normed, 0, 1).astype(BF)
    kv_ref[...] = dg(normed, w[:, third : 3 * third], 1, 0).astype(BF)


def project(x, gain, wqkv):
    tokens, width = x.shape
    third = wqkv.shape[1] // 6
    return pl.pallas_call(
        functools.partial(proj_kernel, third=third),
        grid=(2,),
        in_specs=[
            pl.BlockSpec((tokens, width), lambda i: (0, 0)),
            pl.BlockSpec((1, width), lambda i: (0, 0)),
            pl.BlockSpec((width, 3 * third), lambda i: (0, i)),
        ],
        out_specs=[
            pl.BlockSpec((third, tokens), lambda i: (i, 0)),
            pl.BlockSpec((tokens, 2 * third), lambda i: (0, i)),
        ],
        out_shape=[SHAPE((2 * third, tokens), BF), SHAPE((tokens, 4 * third), BF)],
        compiler_params=params(),
        name="project",
    )(x, gain, wqkv)


def attend_kernel(
    qt_ref, k_ref, v_ref, hot_ref, hott_ref, mats_ref, mask_ref,
    p_ref, o_ref, r_ref, kx, qx, vx,
):
    tokens = k_ref.shape[0]

    @pl.when(pl.program_id(0) == 0)
    def _():
        kx[:, 64:256] = hot_ref[...]
        vx[64:80, :] = jnp.ones((16, tokens), BF)

    vt = v_ref[...].T
    for h in range(2):
        span = slice(64 * h, 64 * h + 64)
        kx[:, 0:64] = k_ref[:, span]
        qx[0:64, :] = qt_ref[span, :] * BF(0.125)
        qx[64:256, :] = dg(mats_ref[h], hott_ref[...], 1, 0).astype(BF)
        vx[0:64, :] = vt[span, :]
        s = dg(kx[...], qx[...], 1, 0) + mask_ref[...]
        top = jnp.max(s, axis=0, keepdims=True)
        p = jnp.exp(s - top).astype(BF)
        p_ref[h] = p
        o = dg(vx[...], p, 1, 0)
        r = 1.0 / o[64:65, :]
        o_ref[span, :] = (o[0:64] * r).astype(BF)
        r_ref[0, h : h + 1, :] = r


def attend(qt, kv, hot, hott, mats, mask):
    channels, tokens = qt.shape
    pairs = channels // 128
    half = pairs // 2
    whole = lambda shape: pl.BlockSpec(shape, lambda i: (0,) * len(shape))
    return pl.pallas_call(
        attend_kernel,
        grid=(pairs,),
        in_specs=[
            pl.BlockSpec((128, tokens), lambda i: (i, 0)),
            pl.BlockSpec((tokens, 128), lambda i: (0, (i // half) * 2 * half + i % half)),
            pl.BlockSpec((tokens, 128), lambda i: (0, (i // half) * 2 * half + half + i % half)),
            whole((tokens, 192)),
            whole((96, tokens)),
            pl.BlockSpec((2, 192, 96), lambda i: (i, 0, 0)),
            whole((tokens, tokens)),
        ],
        out_specs=[
            pl.BlockSpec((2, tokens, tokens), lambda i: (i, 0, 0)),
            pl.BlockSpec((128, tokens), lambda i: (i, 0)),
            pl.BlockSpec((1, 2, tokens), lambda i: (i, 0, 0)),
        ],
        out_shape=[
            SHAPE((2 * pairs, tokens, tokens), BF),
            SHAPE((channels, tokens), BF),
            SHAPE((pairs, 2, tokens), F32),
        ],
        scratch_shapes=[
            pltpu.VMEM((tokens, 256), BF),
            pltpu.VMEM((256, tokens), BF),
            pltpu.VMEM((80, tokens), BF),
        ],
        compiler_params=params(),
        name="attend",
    )(qt, kv, kv, hot, hott, mats, mask)


def attend_back_kernel(
    p_ref, qt_ref, k_ref, v_ref, ot_ref, dot_ref, r_ref, hott_ref, hot_ref,
    dq_ref, dk_ref, dv_ref, gm_ref, vx, dox, kht,
):
    tokens = k_ref.shape[0]

    @pl.when(pl.program_id(0) == 0)
    def _():
        kht[64:160, :] = hott_ref[...]
        lanes = lax.broadcasted_iota(jnp.int32, (tokens, 64), 1)
        vx[:, 64:128] = jnp.where(lanes < 2, -1.0, 0.0).astype(BF)
        dox[64:128, :] = jnp.zeros((64, tokens), BF)

    for h in range(2):
        span = slice(64 * h, 64 * h + 64)
        scaled = dot_ref[span, :].astype(F32) * r_ref[0, h : h + 1, :]
        inner = jnp.sum(scaled * ot_ref[span, :].astype(F32), axis=0, keepdims=True)
        upper = inner.astype(BF)
        lower = (inner - upper.astype(F32)).astype(BF)
        dox[0:64, :] = scaled.astype(BF)
        dox[64:66, :] = jnp.concatenate([upper, lower], 0)
        vx[:, 0:64] = v_ref[:, span]
        kht[0:64, :] = k_ref[:, span].T
        dp = dg(vx[...], dox[...], 1, 0)
        p = p_ref[h]
        ds = (p.astype(F32) * dp).astype(BF)
        dv_ref[:, span] = dg(p, dox[0:64, :], 1, 1).astype(BF)
        dk_ref[:, span] = (dg(ds, qt_ref[span, :], 1, 1) * 0.125).astype(BF)
        both = dg(kht[...], ds, 1, 0)
        dq_ref[:, span] = (both[0:64] * 0.125).astype(BF).T
        left = both[64:160]
        left_hi = left.astype(BF)
        left_lo = (left - left_hi.astype(F32)).astype(BF)
        hot = hot_ref[:, 0:96]
        gm_ref[h] = dg(left_hi, hot, 1, 0) + dg(left_lo, hot, 1, 0)


def attend_back(p, qt, kv, ot, dot, r, hott, hot):
    channels, tokens = qt.shape
    pairs = channels // 128
    half = pairs // 2
    whole = lambda shape: pl.BlockSpec(shape, lambda i: (0,) * len(shape))
    natural = pl.BlockSpec((tokens, 128), lambda i: (0, i))
    turned = pl.BlockSpec((128, tokens), lambda i: (i, 0))
    return pl.pallas_call(
        attend_back_kernel,
        grid=(pairs,),
        in_specs=[
            pl.BlockSpec((2, tokens, tokens), lambda i: (i, 0, 0)),
            turned,
            pl.BlockSpec((tokens, 128), lambda i: (0, (i // half) * 2 * half + i % half)),
            pl.BlockSpec((tokens, 128), lambda i: (0, (i // half) * 2 * half + half + i % half)),
            turned,
            turned,
            pl.BlockSpec((1, 2, tokens), lambda i: (i, 0, 0)),
            whole((96, tokens)),
            whole((tokens, 192)),
        ],
        out_specs=[natural, natural, natural, pl.BlockSpec((2, 96, 96), lambda i: (i, 0, 0))],
        out_shape=[SHAPE((tokens, channels), BF)] * 3 + [SHAPE((2 * pairs, 96, 96), F32)],
        scratch_shapes=[
            pltpu.VMEM((tokens, 128), BF),
            pltpu.VMEM((128, tokens), BF),
            pltpu.VMEM((160, tokens), BF),
        ],
        compiler_params=params(),
        name="attend_back",
    )(p, qt, kv, kv, ot, dot, r, hott, hot)


def middle_kernel(
    x_ref, mixt_ref, wo_ref, dy_ref, gain_ref, wup_ref, wdn_ref,
    y_ref, gup_ref, gdn_ref, gwo_ref, dh_ref, dmt_ref, gg_ref,
    h1, n2, n2t, yacc, dn,
):
    step = pl.program_id(0)

    @pl.when(step == 0)
    def _():
        added = dg(mixt_ref[...], wo_ref[...], 0, 0)
        h = x_ref[...].astype(F32) + added
        h1[...] = h
        yacc[...] = added
        inverse = lax.rsqrt(jnp.mean(h * h, axis=-1, keepdims=True) + EPS)
        normed = (h * inverse * gain_ref[...]).astype(BF)
        n2[...] = normed
        n2t[...] = normed.T
        dn[...] = jnp.zeros_like(dn)

    wup, wdn, dy = wup_ref[...], wdn_ref[...], dy_ref[...]
    u = dg(n2[...], wup, 1, 0)
    cdf = 0.5 * (1.0 + lax.erf(u * 0.7071067811865476))
    act = (u * cdf).astype(BF)
    grad_act = dg(dy, wdn, 1, 1)
    density = jnp.exp(u * u * (-0.5)) * 0.3989422804014327
    du = (grad_act * (cdf + u * density)).astype(BF)
    yacc[...] += dg(act, wdn, 1, 0)
    dn[...] += dg(du, wup, 1, 1)
    gup_ref[...] = dg(n2t[...], du, 1, 0).astype(BF)
    gdn_ref[...] = dg(act, dy, 0, 0).astype(BF)

    @pl.when(step == pl.num_programs(0) - 1)
    def _():
        h = h1[...]
        inverse = lax.rsqrt(jnp.mean(h * h, axis=-1, keepdims=True) + EPS)
        normed = h * inverse
        grad = dn[...]
        gg_ref[...] = jnp.sum(grad * normed, axis=0, keepdims=True)
        inner = grad * gain_ref[...]
        added = inverse * (inner - normed * jnp.mean(inner * normed, axis=-1, keepdims=True))
        dh_ref[...] = added
        y_ref[...] = yacc[...].astype(BF)
        low = (dy_ref[...].astype(F32) + added).astype(BF)
        gwo_ref[...] = dg(low, mixt_ref[...], 0, 1).astype(BF)
        dmt_ref[...] = dg(wo_ref[...], low, 1, 1).astype(BF)


def middle(x, mixt, wo, dy, gain, wup, wdn, chunk=512):
    tokens, width = x.shape
    hidden = wup.shape[1]
    whole = lambda shape: pl.BlockSpec(shape, lambda i: (0,) * len(shape))
    return pl.pallas_call(
        middle_kernel,
        grid=(hidden // chunk,),
        in_specs=[
            whole((tokens, width)),
            whole((width, tokens)),
            whole((width, width)),
            whole((tokens, width)),
            whole((1, width)),
            pl.BlockSpec((width, chunk), lambda i: (0, i)),
            pl.BlockSpec((chunk, width), lambda i: (i, 0)),
        ],
        out_specs=[
            whole((tokens, width)),
            pl.BlockSpec((width, chunk), lambda i: (0, i)),
            pl.BlockSpec((chunk, width), lambda i: (i, 0)),
            whole((width, width)),
            whole((tokens, width)),
            whole((width, tokens)),
            whole((1, width)),
        ],
        out_shape=[
            SHAPE((tokens, width), BF),
            SHAPE((width, hidden), BF),
            SHAPE((hidden, width), BF),
            SHAPE((width, width), BF),
            SHAPE((tokens, width), F32),
            SHAPE((width, tokens), BF),
            SHAPE((1, width), F32),
        ],
        scratch_shapes=[
            pltpu.VMEM((tokens, width), F32),
            pltpu.VMEM((tokens, width), BF),
            pltpu.VMEM((width, tokens), BF),
            pltpu.VMEM((tokens, width), F32),
            pltpu.VMEM((tokens, width), F32),
        ],
        compiler_params=params(60),
        name="middle",
    )(x, mixt, wo, dy, gain, wup, wdn)


def finish_kernel(
    x_ref, gain_ref, dh_ref, dq_ref, dk_ref, dv_ref, w_ref,
    gw_ref, gin_ref, gg_ref, n1, dn, *, third,
):
    step = pl.program_id(0)
    x = x_ref[...].astype(F32)

    @pl.when(step == 0)
    def _():
        inverse = lax.rsqrt(jnp.mean(x * x, axis=-1, keepdims=True) + EPS)
        n1[...] = (x * inverse * gain_ref[...]).astype(BF)
        dn[...] = jnp.zeros_like(dn)

    w = w_ref[...]
    total = dn[...]
    for j, ref in enumerate((dq_ref, dk_ref, dv_ref)):
        span = slice(j * third, (j + 1) * third)
        gw_ref[:, span] = dg(n1[...], ref[...], 0, 0).astype(BF)
        total = total + dg(ref[...], w[:, span], 1, 1)
    dn[...] = total

    @pl.when(step == pl.num_programs(0) - 1)
    def _():
        inverse = lax.rsqrt(jnp.mean(x * x, axis=-1, keepdims=True) + EPS)
        normed = x * inverse
        gg_ref[...] = jnp.sum(total * normed, axis=0, keepdims=True)
        inner = total * gain_ref[...]
        added = inverse * (inner - normed * jnp.mean(inner * normed, axis=-1, keepdims=True))
        gin_ref[...] = (dh_ref[...] + added).astype(BF)


def finish(x, gain, dh, dq, dk, dv, wqkv):
    tokens, width = x.shape
    third = wqkv.shape[1] // 6
    whole = lambda shape: pl.BlockSpec(shape, lambda i: (0,) * len(shape))
    part = pl.BlockSpec((tokens, third), lambda i: (0, i))
    return pl.pallas_call(
        functools.partial(finish_kernel, third=third),
        grid=(2,),
        in_specs=[
            whole((tokens, width)),
            whole((1, width)),
            whole((tokens, width)),
            part,
            part,
            part,
            pl.BlockSpec((width, 3 * third), lambda i: (0, i)),
        ],
        out_specs=[
            pl.BlockSpec((width, 3 * third), lambda i: (0, i)),
            whole((tokens, width)),
            whole((1, width)),
        ],
        out_shape=[
            SHAPE((width, 6 * third), BF),
            SHAPE((tokens, width), BF),
            SHAPE((1, width), F32),
        ],
        scratch_shapes=[pltpu.VMEM((tokens, width), BF), pltpu.VMEM((tokens, width), F32)],
        compiler_params=params(),
        name="finish",
    )(x, gain, dh, dq, dk, dv, wqkv)


def reduce_kernel(y, gin, small, gqkv, gwo, gup, gdn, *rest, n_dp):
    (yret, gret, small_out, fqkv, fwo, fup, fdn) = rest[:7]
    grads = (gqkv, gwo, gup, gdn)
    finals = (fqkv, fwo, fup, fdn)
    rc, ry, rx, rz = rest[7:11], rest[11:15], rest[15:19], rest[19:23]
    sums, got = rest[23:25]
    far = rest[25:29] if n_dp > 16 else None
    send, recv = rest[-2:]
    links = Links(send, recv)
    d, m = links.d, links.m
    bits = n_dp.bit_length() - 1
    flips = [(0, 1)] + [(1 << b, 0) for b in range(bits)] + [(12, 0)]
    flips += [(r << 4, 0) for r in range(1, n_dp // 16) if r & (r - 1)]
    links.barrier(flips)
    core, cross, deep = d & 1, (d >> 1) & 1, (d >> 2) & 3
    rows = y.shape[0] // 2
    started = []

    def go(copy):
        copy.start()
        started.append(copy)
        return copy

    mine = rows_at(m * rows, rows, rows)
    theirs = rows_at((1 - m) * rows, rows, rows)
    locals_ = [links.local(y.at[mine], yret.at[m]), links.local(gin.at[mine], gret.at[m])]
    for copy in locals_:
        copy.start()

    def half(i, side, start, count, ref, based):
        own = finals[i].shape
        if i == 3:
            base = side * own[0] if based else 0
            return ref.at[rows_at(base + start, count, 16)]
        cols = slice(side * own[1], (side + 1) * own[1])
        return ref.at[rows_at(start, count, 16), cols]

    order = (3, 2, 0, 1)
    size = [f.shape[0] for f in finals]
    copies = {}

    def start_core(i):
        n = size[i] // 2
        for side in range(2):
            src = half(i, side, (1 - core) * n, n, grads[i], True)
            copies["c", i, side] = go(links.remote(src, rc[i].at[side], dp_flip=1))

    def start_y(i):
        n = size[i] // 2
        for side in range(2):
            copies["c", i, side].wait_recv()
            src = half(i, side, core * n, n, grads[i], True)
            rc[i][side] = (rc[i][side].astype(F32) + src[...].astype(F32)).astype(BF)
        copies["y", i] = go(links.remote(rc[i].at[1], ry[i], mp_flip=1))

    def start_x(i):
        n = size[i] // 4
        copies["y", i].wait_recv()
        ry[i][...] = (ry[i][...].astype(F32) + rc[i][0].astype(F32)).astype(BF)
        src = ry[i].at[rows_at((1 - cross) * n, n, 16)]
        copies["x", i] = go(links.remote(src, rx[i], dp_flip=2))

    def start_z(i):
        n = size[i] // 16
        copies["x", i].wait_recv()
        keep = ry[i][rows_at(cross * size[i] // 4, size[i] // 4, 16)]
        rx[i][...] = (rx[i][...].astype(F32) + keep.astype(F32)).astype(BF)
        for r in range(1, 4):
            src = rx[i].at[rows_at((deep ^ r) * n, n, 16)]
            copies["z", i, r] = go(links.remote(src, rz[i].at[r - 1], dp_flip=r << 2))

    def place(i, count):
        n = size[i] // 16
        at = {1: core * 8 + cross * 4 + deep, 4: core * 8 + cross * 4, 8: core * 8}[count]
        return finals[i].at[rows_at(at * n, count * n, 16)]

    def start_back_z(i):
        n = size[i] // 16
        for r in range(1, 4):
            copies["z", i, r].wait_recv()
        total = rx[i][rows_at(deep * n, n, 16)].astype(F32)
        for r in range(3):
            total = total + rz[i][r].astype(F32)
        if far is not None:
            rz_own = far[i]
            rz_own[0] = total.astype(BF)
            group = [
                go(links.remote(rz_own.at[0], rz_own.at[r], dp_flip=r << 4))
                for r in range(1, n_dp // 16)
            ]
            for r, copy in enumerate(group):
                copy.wait_recv()
                total = total + rz_own[r + 1].astype(F32)
        spot = place(i, 1)
        spot[...] = total.astype(BF)
        for r in range(1, 4):
            copies["bz", i, r] = go(links.remote(spot, spot, dp_flip=r << 2))

    def start_back_x(i):
        for r in range(1, 4):
            copies["bz", i, r].wait_recv()
        spot = place(i, 4)
        copies["bx", i] = go(links.remote(spot, spot, dp_flip=2))

    def start_back_c(i):
        copies["bx", i].wait_recv()
        spot = place(i, 8)
        copies["bc", i] = go(links.remote(spot, spot, dp_flip=1))

    def end(i):
        copies["bc", i].wait_recv()

    stages = (start_core, start_y, start_x, start_z, start_back_z, start_back_x, start_back_c, end)
    sums[0] = small[...]
    n_small = bits + 1
    tick = 0
    for t in range(len(stages) + len(order) - 1):
        for j, i in enumerate(order):
            if 0 <= t - j < len(stages):
                stages[t - j](i)
        if t == 3:
            row_copies = [
                go(links.remote(y.at[theirs], yret.at[m], mp_flip=1)),
                go(links.remote(gin.at[theirs], gret.at[m], mp_flip=1)),
            ]
        if tick <= n_small:
            if tick > 0:
                hop.wait_recv()
                if tick == 1:
                    sums[1, 0:16] = sums[0, 0:16] + got[0, 0:16]
                    sums[1, 16:24] = sums[0, 16:24] + got[0, 24:32]
                    sums[1, 24:32] = jnp.zeros_like(sums[0, 24:32])
                else:
                    sums[tick] = sums[tick - 1] + got[tick - 1]
            if tick < n_small:
                flip = (0, 1) if tick == 0 else (1 << (tick - 1), 0)
                hop = go(links.remote(sums.at[tick], got.at[tick], dp_flip=flip[0], mp_flip=flip[1]))
            tick += 1
    small_out[...] = sums[n_small]
    for copy in row_copies:
        copy.wait_recv()
    for copy in started:
        copy.wait_send()
    for copy in locals_:
        copy.wait()


def reduce_all(y, gin, small, gqkv, gwo, gup, gdn, n_dp):
    tokens, width = y.shape
    own = (
        (width, gqkv.shape[1] // 2),
        (width, gwo.shape[1] // 2),
        (width, gup.shape[1] // 2),
        (gdn.shape[0] // 2, width),
    )
    bits = n_dp.bit_length() - 1
    scratch = [pltpu.VMEM((2, a // 2, b), BF) for a, b in own]
    scratch += [pltpu.VMEM((a // 2, b), BF) for a, b in own]
    scratch += [pltpu.VMEM((a // 4, b), BF) for a, b in own]
    scratch += [pltpu.VMEM((3, a // 16, b), BF) for a, b in own]
    scratch += [pltpu.VMEM((bits + 2,) + small.shape, F32)] * 2
    count = 80
    if n_dp > 16:
        scratch += [pltpu.VMEM((n_dp // 16, a // 16, b), BF) for a, b in own]
        count += 4 * (n_dp // 16)
    scratch += [pltpu.SemaphoreType.DMA((count,))] * 2
    return pl.pallas_call(
        functools.partial(reduce_kernel, n_dp=n_dp),
        out_shape=[
            SHAPE((2, tokens // 2, width), BF),
            SHAPE((2, tokens // 2, width), BF),
            SHAPE(small.shape, F32),
        ]
        + [SHAPE(s, BF) for s in own],
        in_specs=[ANY, ANY] + [VMEM] * 5,
        out_specs=[ANY, ANY] + [VMEM] * 5,
        scratch_shapes=scratch,
        compiler_params=params(60, collective_id=2, has_side_effects=True),
        name="reduce",
    )(y, gin, small, gqkv, gwo, gup, gdn)


def local(
    n_dp, inputs, roi, cotangent, doc_lengths, live_mask, bucket_cells,
    gain_attn, gain_ffn, w_query, w_key, w_value, w_out, w_up, w_down, tables,
):
    rows, width = inputs.shape[1], inputs.shape[2]
    tokens = 2 * rows
    third = w_query.shape[1]
    heads = third // HDIM
    buckets = tables.shape[1]
    half = buckets // 2
    m = lax.axis_index("mp")

    resid = inputs.astype(F32) + roi.astype(F32)
    tab = jnp.pad(
        tables.transpose(2, 0, 1).reshape(heads, 3 * buckets), ((0, 2), (0, 128 - 3 * buckets))
    )
    x, dy, tab_other, wqkv, wo, wup, wdn = gather(
        resid.astype(BF), cotangent, tab, w_query, w_key, w_value, w_out, w_up, w_down
    )

    lengths = lax.dynamic_index_in_dim(doc_lengths, m, 0, keepdims=False)[0]
    live = lax.dynamic_index_in_dim(live_mask, m, 0, keepdims=False)
    cells = lax.dynamic_index_in_dim(bucket_cells, m, 0, keepdims=False)
    ids = jnp.arange(tokens)
    segment = jnp.sum((ids[:, None] >= jnp.cumsum(lengths)[None, :]).astype(jnp.int32), axis=1)
    allowed = (segment[:, None] == segment[None, :]) & (
        (live[:, None] == 1) | (ids[:, None] == ids[None, :])
    )
    mask = jnp.where(allowed, 0.0, MASKED).astype(F32)
    cell_ids = jnp.arange(buckets)
    hott = (cells[:, None, :] == cell_ids[None, :, None]).astype(BF).reshape(3 * buckets, tokens)
    hot = (cells.T[:, :, None] == cell_ids[None, None, :]).astype(BF).reshape(tokens, 3 * buckets)
    hot = jnp.concatenate([hot, hot], axis=1)
    relative = jnp.clip(cell_ids[:, None] - cell_ids[None, :], -half, half - 1) + half
    select = (relative[:, :, None] == cell_ids).astype(F32)
    both = jnp.concatenate([tab[:heads], tab_other[:heads]], 0)[:, : 3 * buckets]
    both = both.reshape(2 * heads, 3, buckets)
    blocks = jnp.einsum("han,xyn->haxy", both, select, precision=lax.Precision.HIGHEST)
    eye = jnp.eye(3, dtype=F32)
    mats = (blocks[:, :, :, None, :] * eye[None, :, None, :, None]).reshape(
        2 * heads, 3 * buckets, 3 * buckets
    )
    mats_hi = mats.astype(BF)
    mats_lo = (mats - mats_hi.astype(F32)).astype(BF)
    mats = jnp.concatenate([mats_hi, mats_lo], axis=1)

    ga, gf = gain_attn.reshape(1, width), gain_ffn.reshape(1, width)
    qt, kv = project(x, ga, wqkv)
    p, mixt, r = attend(qt, kv, hot, hott, mats, mask)
    y, gup, gdn, gwo, dh, dmt, gain_f = middle(x, mixt, wo, dy, gf, wup, wdn)
    dq, dk, dv, gmats = attend_back(p, qt, kv, mixt, dmt, r, hott, hot)
    gqkv, gin, gain_a = finish(x, ga, dh, dq, dk, dv, wqkv)

    gblocks = jnp.stack(
        [gmats[:, t * buckets : (t + 1) * buckets, t * buckets : (t + 1) * buckets] for t in range(3)],
        axis=1,
    )
    gtab = jnp.einsum("haxy,xyn->han", gblocks, select, precision=lax.Precision.HIGHEST)
    gtab = jnp.pad(
        gtab.reshape(2, heads, 3 * buckets), ((0, 0), (0, 2), (0, 128 - 3 * buckets))
    ).reshape(16, 128)
    small = jnp.concatenate(
        [gain_a.reshape(-1, 128), gain_f.reshape(-1, 128), jnp.zeros((4, 128), F32), gtab], 0
    )
    yret, gret, small, fqkv, fwo, fup, fdn = reduce_all(y, gin, small, gqkv, gwo, gup, gdn, n_dp)
    lines = width // 128
    out = resid + yret.astype(F32)
    grad_in = cotangent.astype(F32) + gret.astype(F32)
    table_out = small[16 : 16 + heads, : 3 * buckets].reshape(heads, 3, buckets).transpose(1, 2, 0)
    return (
        out,
        grad_in,
        small[0:lines].reshape(width),
        small[lines : 2 * lines].reshape(width),
        fqkv[:, 0:third].astype(F32),
        fqkv[:, third : 2 * third].astype(F32),
        fqkv[:, 2 * third :].astype(F32),
        fwo.T.astype(F32),
        fup.astype(F32),
        fdn.astype(F32),
        table_out,
    )


def solution(mesh):
    n_dp = mesh.shape["dp"]
    rows = P(None, ("dp", "mp"), None)
    columns, lines = P(None, "mp"), P("mp", None)
    tables = P(None, None, "mp")
    return jax.shard_map(
        functools.partial(local, n_dp),
        mesh=mesh,
        in_specs=(
            rows, rows, rows, P(None, "dp", None), P(None, "dp"), P(None, None, "dp"),
            P(), P(), columns, columns, columns, lines, columns, lines, tables,
        ),
        out_specs=(
            rows, rows, P(), P(), columns, columns, columns, lines, columns, lines, tables,
        ),
        check_vma=False,
    )
```

time: 1410 us -> 448 us (0.32)
  matrix products: 577 us -> 2.2 us
  waiting for transfers between devices: 472 us -> 0 us
  Pallas kernels: 0 us -> 383 us
  blocking collectives: 103 us -> 0 us
  other arithmetic: 118 us -> 25.7 us
  local copies, waits for them, and re-layouts: 100 us -> 28.2 us
  loops' own time: 14.7 us -> 0 us
    dot_general x94 -> x2, matrix products: 577 us -> 2.2 us  [the longest x1 1.42 us: local(): jnp.einsum('han,xyn->haxy', both, select, precision=lax.Precision.HIGHEST)]
    pallas_call x0 -> x7, Pallas kernels: none -> 383 us  [the longest x1 166 us: reduce_all(): pl.pallas_call(functools.partial(reduce_kernel, n_dp=n_dp), out_shape=[SH...]
    psum x1 -> x0, waiting for transfers between devices: 164 us -> none  [local(): lax.psum((acc_proj, acc_out, acc_up, acc_down, table_grad), 'dp')]
    all_gather x8 -> x0, waiting for transfers between devices: 158 us -> none  [the longest x2 51.2 us: local(): expand_piece = lax.all_gather(normed_ffn, 'mp', axis=0, tiled=True)]
    reduce_scatter x8 -> x0, waiting for transfers between devices: 148 us -> none  [the longest x2 79.5 us: local(): lax.psum_scatter(jnp.einsum('tf,df->td', lax.slice_in_dim(grad_pre, 0, lo...]
    psum x2 -> x0, blocking collectives: 103 us -> none  [the longest x1 63.4 us: local(): lax.psum((acc_proj, acc_out, acc_up, acc_down, table_grad), 'dp')]
    reduce_sum x11 -> x1, other arithmetic: 48.5 us -> 0.08 us  [local(): jnp.sum((ids[:, None] >= jnp.cumsum(lengths)[None, :]).astype(jnp.int32),...]
    convert_element_type x37 -> x7, other arithmetic: 40.2 us -> 12.5 us  [the longest x1 3.88 us: local(): fqkv[:, 2 * third:].astype(F32)]
  transfers between devices with their start and end apart: 17 -> 0, of which waited for: 13 -> 0; matrix products, arithmetic and copies ran while one was open for 29% -> 0% of each run, Pallas kernels for 0% -> 0%
where the time goes in v1:
time: 448 us; the launch traced here: 440 us
  Pallas kernels  383 us (85%)
  local copies, waits for them, and re-layouts  28.2 us (6%)
  other arithmetic  25.7 us (6%)
    pallas_call x1, Pallas kernels, reduce_all(): pl.pallas_call(functools.partial(reduce_kernel, n_dp=n_dp), out_shape=[SH...  166 us
    pallas_call x1, Pallas kernels, gather(): pl.pallas_call(gather_kernel, out_shape=[SHAPE((2 * rows, width), BF), SH...  83.3 us
    pallas_call x1, Pallas kernels, middle(): pl.pallas_call(middle_kernel, grid=(hidden // chunk,), in_specs=[whole((t...  44.5 us
    pallas_call x1, Pallas kernels, attend_back(): pl.pallas_call(attend_back_kernel, grid=(pairs,), in_specs=[pl.BlockSpec(...  32 us
    pallas_call x1, Pallas kernels, attend(): pl.pallas_call(attend_kernel, grid=(pairs,), in_specs=[pl.BlockSpec((128,...  30.3 us
    pallas_call x1, Pallas kernels, finish(): pl.pallas_call(functools.partial(finish_kernel, third=third), grid=(2,),...  18.5 us
    unnamed x50, local copies, waits for them, and re-layouts  18 us

profile of v1, /device:TPU:0, one launch (start us, length us, event | category | flops | bytes accessed | tf_op | source)
XLA Modules:
  0.0 439.9 jit_solution(3217872158019226610)
XLA Ops:
  0.6 0.0 copy-start
  0.7 0.7 copy.49
  1.4 0.1 reshape.128
  1.5 0.0 copy-start.11
  1.5 2.4 fusion.3.hi
  3.9 0.0 copy-done.4
  3.9 0.7 copy-done.7
  4.6 0.1 copy-done.11
  4.7 1.7 copy-done.8
  6.3 1.1 copy-done.12
  7.4 1.1 copy-done.13
  8.5 1.1 copy-done.14
  9.5 83.3 %gather.1 = (bf16[1024,768]{1,0:T(8,128)(2,1)S(1)}, bf16[1024,768]{1,0:T(8,128)(2,1)S(1)}, f32[8,128]{1,0:T(8,128)S(1)}, bf16[768,2304]{1,0:T(8,128)(2,1)S(1)}, ...) custom-call(bf16[2,512,768]{2,1,0:T(8,128)(2,1)S(1)} %fusion.3.hi, ...), custom_call_target="tpu_custom_call" | custom-call | tf_op jit(solution)/shard_map/gather/pallas_call | solution.py:165
  92.8 0.0 copy-start.2
  92.8 1.8 copy-done.2
  94.6 1.1 copy-done.3
  95.8 2.2 copy-done.5
  98.0 2.2 copy-done.6
  100.2 1.2 copy-done.9
  101.3 1.0 copy-done.10
  102.3 0.1 reshape.130
  102.4 1.4 fusion.7
  103.9 0.2 copy.53
  104.1 1.8 mul.20
  105.9 2.8 mul.21
  108.7 0.0 copy-start.19
  108.7 0.1 mul.22
  108.8 0.1 mul.23
  109.0 0.1 multiply_convert_fusion
  109.1 1.0 pad_maximum_fusion.mats_ref
  110.0 0.0 copy-done.19
  110.0 0.6 reshape.129.g_ref.gain_ref
  110.6 7.6 %project.1 = (bf16[768,1024]{1,0:T(8,128)(2,1)}, bf16[1024,1536]{1,0:T(8,128)(2,1)}) custom-call(bf16[1024,768]{1,0:T(8,128)(2,1)} %copy-done.3, f32[1,768]{1,0:T(1,128)} %reshape.129.g_ref.gain_ref, bf16[768,2304]{1,0:T(8,128)(2,1)} %copy-done.2), custom_call_target="tpu_custom_call" | custom-call | tf_op jit(solution)/shard_map/project/pallas_call | solution.py:196
  118.2 0.0 copy-done.23
  118.2 0.2 reduce-window.8
  118.4 0.1 convert_reduce_fusion
  118.5 0.0 copy-done.22
  118.6 2.8 fusion.2.mask_ref
  121.4 0.2 copy.50
  121.6 0.1 eq.109
  121.7 0.1 broadcast_compare_fusion
  121.8 1.1 add_convert_fusion.hot_ref
  122.9 0.8 fusion.9.hott_ref
  123.7 30.3 %attend.1 = (bf16[12,1024,1024]{2,1,0:T(8,128)(2,1)}, bf16[768,1024]{1,0:T(8,128)(2,1)}, f32[6,2,1024]{2,1,0:T(2,128)}) custom-call(bf16[768,1024]{1,0:T(8,128)(2,1)} %get-tuple-element.46.qt_ref, bf16[1024,1536]{1,0:T(8,128)(2,1)} %get-tuple-element.47.k_ref.v_ref, bf16[1024,1536]{1,0:T(8,128)(2,1)} %get-tuple-element.47.k_ref.v_ref, ...), custom_call_target="tpu_custom_call" | custom-call | tf_op jit(solution)/shard_map/attend/pallas_call | solution.py:247
  154.1 0.6 reshape.133.gain_ref
  154.7 44.5 %middle.1 = (bf16[1024,768]{1,0:T(8,128)(2,1)}, bf16[768,3072]{1,0:T(8,128)(2,1)}, bf16[3072,768]{1,0:T(8,128)(2,1)}, bf16[768,768]{1,0:T(8,128)(2,1)}, f32[1024...) custom-call(bf16[1024,768]{1,0:T(8,128)(2,1)} %copy-done.3, ...), custom_call_target="tpu_custom_call" | custom-call | tf_op jit(solution)/shard_map/middle/pallas_call | solution.py:400
  199.2 32.0 %attend_back.1 = (bf16[1024,768]{1,0:T(8,128)(2,1)}, bf16[1024,768]{1,0:T(8,128)(2,1)}, bf16[1024,768]{1,0:T(8,128)(2,1)}, f32[12,96,96]{2,1,0:T(8,128)}) custom-call(bf16[12,1024,1024]{2,1,0:T(8,128)(2,1)} %get-tuple-element.56.p_ref, bf16[768,1024]{1,0:T(8,128)(2,1)} %get-tuple-element.46.qt_ref, bf16[1024,1536]{1,0:T(8,128)(2,1)} %get-tuple-element.47.k_ref.v_ref, ...), custom_call_target="tpu_custom_call" | custom-call | tf_op jit(solution)/shard_map/attend_back/pallas_call | solution.py:323
  231.2 1.3 slice_bitcast_fusion.2
  232.5 0.1 pad_maximum_fusion.1
  232.6 0.8 convolution_bitcast_fusion
  233.4 0.1 reshape.136
  233.5 18.5 %finish.1 = (bf16[768,2304]{1,0:T(8,128)(2,1)}, bf16[1024,768]{1,0:T(8,128)(2,1)}, f32[1,768]{1,0:T(1,128)}) custom-call(bf16[1024,768]{1,0:T(8,128)(2,1)} %copy-done.3, f32[1,768]{1,0:T(1,128)} %reshape.129.g_ref.gain_ref, f32[1024,768]{1,0:T(8,128)} %get-tuple-element.55.dh_ref, bf16[1024,768]{1,0:T(8,128)(2,1)} %get-tuple-element.59.dq_ref, ...), custom_call_target="tpu_custom_call" | custom-call | tf_op jit(solution)/shard_map/finish/pallas_call | solution.py:478
  252.0 0.7 reduce.2
  252.8 0.1 pad.12.clone
  252.8 0.7 pad_maximum_fusion.2.small
  253.5 166.2 %reduce.5 = (bf16[2,512,768]{2,1,0:T(8,128)(2,1)}, bf16[2,512,768]{2,1,0:T(8,128)(2,1)}, f32[32,128]{1,0:T(8,128)}, bf16[768,1152]{1,0:T(8,128)(2,1)}, bf16[768,...) custom-call(bf16[1024,768]{1,0:T(8,128)(2,1)} %get-tuple-element.54.y, ...), custom_call_target="tpu_custom_call" | custom-call | tf_op jit(solution)/shard_map/reduce/pallas_call | solution.py:672
  419.7 3.9 slice_convert_fusion
  423.6 2.8 copy.57
  426.4 6.4 %convert_add_fusion = (f32[2,512,768]{2,1,0:T(8,128)}, f32[2,512,768]{2,1,0:T(8,128)}) fusion(bf16[2,512,768]{2,1,0:T(8,128)(2,1)} %get-tuple-element.71, bf16[2,512,768]{2,1,0:T(8,128)(2,1)S(1)} %copy-done.4, bf16[2,512,768]{2,1,0:T(8,128)(2,1)} %get-tuple-element.70, bf16[2,512,768]{2,1,0:T(8,128)(2,1)S(1)} %copy-done.15, bf16[2,512,768]{2,1,0:T(8,128)(2,1)} %param.15), kind=kLoop, calls=%fused_computation.4 | loop fusion | flops 6291456 | bytes 14155776 | tf_op jit(solution)/shard_map/add | solution.py:755
  432.8 2.8 convert_element_type.86
  435.6 2.5 convert_element_type.87
  438.2 0.1 reshape.140
  438.2 0.6 copy.71
  438.9 0.6 slice_bitcast_fusion.3
  (44 shorter events, 0.2 us)
Async XLA Ops:
  0.6 120.7 %copy-start = (s32[2,3,1024]{2,0,1:T(2,128)S(1)}, s32[2,3,1024]{2,0,1:T(2,128)}, u32[]{:S(2)}) copy-start(s32[2,3,1024]{2,0,1:T(2,128)} %param.20) | copy-start | bytes 73732
  1.5 2.4 copy-start.4
  1.5 3.1 copy-start.7
  1.5 3.2 copy-start.11
  4.7 1.7 copy-start.8
  6.3 1.1 copy-start.12
  7.4 1.1 copy-start.13
  8.5 1.1 copy-start.14
  92.8 1.8 copy-start.2
  94.6 1.1 copy-start.3
  95.8 2.2 copy-start.5
  98.0 2.2 copy-start.6
  100.1 1.2 copy-start.9
  101.3 1.0 copy-start.10
  108.7 1.3 copy-start.19
  110.6 7.6 %copy-start.23 = (s32[2,1,8]{2,1,0:T(1,128)S(1)}, s32[2,1,8]{2,1,0:T(1,128)}, u32[]{:S(2)}) copy-start(s32[2,1,8]{2,1,0:T(1,128)} %param.18) | copy-start | bytes 196
  110.6 7.9 %copy-start.22 = (s32[2,1024]{1,0:T(2,128)S(1)}, s32[2,1024]{1,0:T(2,128)}, u32[]{:S(2)}) copy-start(s32[2,1024]{1,0:T(2,128)} %param.19) | copy-start | bytes 24580
  123.7 30.3 %copy-start.20 = (f32[768]{0:T(1024)S(1)}, f32[768]{0:T(1024)}, u32[]{:S(2)}) copy-start(f32[768]{0:T(1024)} %param.22) | copy-start | bytes 9220
  233.5 19.3 %copy-start.21 = (f32[1,768]{1,0:T(1,128)S(1)}, f32[1,768]{1,0:T(1,128)}, u32[]{:S(2)}) copy-start(f32[1,768]{1,0:T(1,128)} %get-tuple-element.64) | copy-start | bytes 9220
  423.6 2.8 copy-start.15
  426.4 6.4 %copy-start.17 = (bf16[768,1536]{1,0:T(8,128)(2,1)S(1)}, bf16[768,1536]{1,0:T(8,128)(2,1)}, u32[]{:S(2)}) copy-start(bf16[768,1536]{1,0:T(8,128)(2,1)} %get-tuple-element.75) | copy-start | bytes 7077892
  432.8 2.8 copy-start.16
  435.6 2.6 copy-start.18
  435.6 3.8 copy-start.1

commit v2 on v1

--- a/solution.py
+++ b/solution.py
@@ -15,7 +15,7 @@
 MASKED = -1e30
 MESH = pl.DeviceIdType.MESH
 VMEM = pl.BlockSpec(memory_space=pltpu.VMEM)
-ANY = pl.BlockSpec(memory_space=pl.ANY)
+ANY = pl.BlockSpec(memory_space=pltpu.HBM)
 SHAPE = jax.ShapeDtypeStruct
 
 
@@ -64,172 +64,260 @@
     return pl.ds(pl.multiple_of(start, unit), size)
 
 
-def gather_kernel(
-    hi, cot, tab, wq, wk, wv, wo, wup, wdn,
-    xf, dyf, tabo, qkvf, wof, wupf, wdnf,
-    send, recv,
+def entry_kernel(
+    inp, roi, tab, gain, wq, wk, wv, wup,
+    xf, tabo, wqkv, qt, kv, upo,
+    sent, n1, send, recv,
 ):
     links = Links(send, recv)
     d, m = links.d, links.m
-    rows = hi.shape[1]
-    width = wq.shape[0]
-    third = wq.shape[1]
-    hidden = wup.shape[1]
-    inner = wo.shape[0]
+    rows = inp.shape[1]
+    width, third = wq.shape
+    piece = width // 8
+    core, cross, deep = d & 1, (d >> 1) & 1, (d >> 2) & 1
+    place = core * 4 + cross * 2 + deep
     links.barrier(((0, 1), (1, 0), (2, 0), (4, 0)))
-    core, cross, deep = d & 1, (d >> 1) & 1, (d >> 2) & 1
-    other = 1 - m
-    locals_ = []
-    own_rows = rows_at(m * rows, rows, rows)
-    waits = []
+    started = []
 
     def go(copy):
         copy.start()
-        waits.append(copy)
+        started.append(copy)
         return copy
 
-    targets = (
-        (qkvf, 0, width, slice(3 * third, 6 * third)),
-        (wof, inner, inner, slice(0, width)),
-        (wupf, 0, width, slice(hidden, 2 * hidden)),
-        (wdnf, hidden, hidden, slice(0, width)),
-    )
-    sources = ((wq, wk, wv), (wo,), (wup,), (wdn,))
-
-    def block(entry, first, count):
-        full, base, total, columns = entry
-        piece = total // 8
-        return full.at[rows_at(base + first * piece, count * piece, piece), columns]
-
-    place = core * 4 + cross * 2 + deep
-    stage_y = []
-    for entry, parts in zip(targets, sources):
-        full, base, total, columns = entry
-        piece = total // 8
-        group = []
-        for j, part in enumerate(parts):
-            span = part.shape[1]
-            cols = slice(columns.start + j * span, columns.start + (j + 1) * span)
-            group.append(
-                go(
-                    links.remote(
-                        part.at[rows_at(place * piece, piece, piece)],
-                        full.at[rows_at(base + place * piece, piece, piece), cols],
-                        mp_flip=1,
-                    )
-                )
-            )
-        stage_y.append(group)
-        if full is qkvf:
-            row_copies = [
-                go(links.remote(tab, tabo, mp_flip=1)),
-                go(links.remote(hi.at[other], xf.at[own_rows], mp_flip=1)),
-            ]
-    row_copies.append(go(links.remote(cot.at[other], dyf.at[own_rows], mp_flip=1)))
-    locals_.append(links.local(hi.at[m], xf.at[own_rows]))
-    locals_.append(links.local(cot.at[m], dyf.at[own_rows]))
-    for j, part in enumerate((wq, wk, wv)):
-        locals_.append(links.local(part, qkvf.at[:, j * third : (j + 1) * third]))
-    locals_.append(links.local(wo, wof.at[0:inner]))
-    locals_.append(links.local(wup, wupf.at[:, 0:hidden]))
-    locals_.append(links.local(wdn, wdnf.at[0:hidden]))
-    for copy in locals_:
-        copy.start()
-    stage = stage_y
-    for flip, first, count in (
+    own_cols = [slice(j * third, (j + 1) * third) for j in range(3)]
+    other_cols = [slice((3 + j) * third, (4 + j) * third) for j in range(3)]
+    spot = rows_at(place * piece, piece, piece)
+    first = [
+        go(links.remote(w.at[spot], wqkv.at[spot, c], mp_flip=1))
+        for w, c in zip((wq, wk, wv), other_cols)
+    ]
+    tab_copy = go(links.remote(tab, tabo, mp_flip=1))
+    chunk = rows // 2
+    row_copies = []
+    for j in range(2):
+        part = slice(j * chunk, (j + 1) * chunk)
+        sent[part] = (inp[1 - m, part].astype(F32) + roi[1 - m, part].astype(F32)).astype(BF)
+        here = rows_at(m * rows + j * chunk, chunk, chunk)
+        row_copies.append(go(links.remote(sent.at[part], xf.at[here], mp_flip=1)))
+    up_copy = go(links.remote(wup.at[spot], upo.at[spot], mp_flip=1))
+    for w, c in zip((wq, wk, wv), own_cols):
+        wqkv[:, c] = w[...]
+
+    def normalise(where):
+        x = xf[where].astype(F32)
+        inverse = lax.rsqrt(jnp.mean(x * x, axis=-1, keepdims=True) + EPS)
+        n1[where] = (x * inverse * gain[...]).astype(BF)
+
+    own = rows_at(m * rows, rows, rows)
+    xf[own] = (inp[m].astype(F32) + roi[m].astype(F32)).astype(BF)
+    normalise(own)
+
+    def project(where, side):
+        rows_in = n1[where]
+        base = side * 3 * third
+        kv[where, side * 2 * third : (side + 1) * 2 * third] = dg(
+            rows_in, wqkv[:, base + third : base + 3 * third], 1, 0
+        ).astype(BF)
+        qt[side * third : (side + 1) * third, where] = dg(
+            wqkv[:, base : base + third], rows_in, 0, 1
+        ).astype(BF)
+
+    project(own, 0)
+    stage = first
+    for flip, begin, count in (
         (4, place, 1),
         (2, core * 4 + cross * 2, 2),
         (1, core * 4, 4),
     ):
-        following = []
-        for entry, group in zip(targets, stage):
-            for copy in group:
-                copy.wait_recv()
-            there = block(entry, first, count)
-            following.append([go(links.remote(there, there, dp_flip=flip))])
-        stage = following
-    for group in stage:
-        for copy in group:
+        for copy in stage:
             copy.wait_recv()
-    for copy in row_copies:
+        there = wqkv.at[rows_at(begin * piece, count * piece, piece), 3 * third : 6 * third]
+        stage = [go(links.remote(there, there, dp_flip=flip))]
+    for j in range(2):
+        row_copies[j].wait_recv()
+        here = rows_at((1 - m) * rows + j * chunk, chunk, chunk)
+        normalise(here)
+        project(here, 0)
+    for copy in stage:
         copy.wait_recv()
-    for copy in waits:
+    for j in range(2):
+        project(slice(j * rows, (j + 1) * rows), 1)
+    tab_copy.wait_recv()
+    up_copy.wait_recv()
+    for copy in started:
         copy.wait_send()
-    for copy in locals_:
-        copy.wait()
-
-
-def gather(hi, cot, tab, wq, wk, wv, wo, wup, wdn):
-    rows, width = hi.shape[1], hi.shape[2]
-    third, hidden = wq.shape[1], wup.shape[1]
+
+
+def entry(inputs, roi, tab, gain, wq, wk, wv, wup):
+    rows, width = inputs.shape[1], inputs.shape[2]
+    third = wq.shape[1]
+    tokens = 2 * rows
     return pl.pallas_call(
-        gather_kernel,
+        entry_kernel,
         out_shape=[
-            SHAPE((2 * rows, width), BF),
-            SHAPE((2 * rows, width), BF),
+            SHAPE((tokens, width), BF),
             SHAPE(tab.shape, F32),
             SHAPE((width, 6 * third), BF),
-            SHAPE((2 * third, width), BF),
-            SHAPE((width, 2 * hidden), BF),
-            SHAPE((2 * hidden, width), BF),
-        ],
-        in_specs=[ANY] * 9,
-        out_specs=[ANY] * 7,
-        scratch_shapes=[pltpu.SemaphoreType.DMA((40,)), pltpu.SemaphoreType.DMA((40,))],
-        compiler_params=params(16, collective_id=1, has_side_effects=True),
-        name="gather",
-    )(hi, cot, tab, wq, wk, wv, wo, wup, wdn)
-
-
-def proj_kernel(x_ref, g_ref, w_ref, q_ref, kv_ref, *, third):
-    x = x_ref[...].astype(F32)
-    inverse = lax.rsqrt(jnp.mean(x * x, axis=-1, keepdims=True) + EPS)
-    normed = (x * inverse * g_ref[...]).astype(BF)
-    w = w_ref[...]
-    q_ref[...] = dg(w[:, 0:third], normed, 0, 1).astype(BF)
-    kv_ref[...] = dg(normed, w[:, third : 3 * third], 1, 0).astype(BF)
-
-
-def project(x, gain, wqkv):
-    tokens, width = x.shape
-    third = wqkv.shape[1] // 6
-    return pl.pallas_call(
-        functools.partial(proj_kernel, third=third),
-        grid=(2,),
-        in_specs=[
-            pl.BlockSpec((tokens, width), lambda i: (0, 0)),
-            pl.BlockSpec((1, width), lambda i: (0, 0)),
-            pl.BlockSpec((width, 3 * third), lambda i: (0, i)),
-        ],
-        out_specs=[
-            pl.BlockSpec((third, tokens), lambda i: (i, 0)),
-            pl.BlockSpec((tokens, 2 * third), lambda i: (0, i)),
-        ],
-        out_shape=[SHAPE((2 * third, tokens), BF), SHAPE((tokens, 4 * third), BF)],
-        compiler_params=params(),
-        name="project",
-    )(x, gain, wqkv)
+            SHAPE((2 * third, tokens), BF),
+            SHAPE((tokens, 4 * third), BF),
+            SHAPE(wup.shape, BF),
+        ],
+        in_specs=[VMEM] * 7 + [ANY],
+        out_specs=[VMEM] * 5 + [ANY],
+        scratch_shapes=[
+            pltpu.VMEM((rows, width), BF),
+            pltpu.VMEM((tokens, width), BF),
+            pltpu.SemaphoreType.DMA((12,)),
+            pltpu.SemaphoreType.DMA((12,)),
+        ],
+        compiler_params=params(58, collective_id=1, has_side_effects=True),
+        name="entry",
+    )(inputs, roi, tab, gain, wq, wk, wv, wup)
 
 
 def attend_kernel(
-    qt_ref, k_ref, v_ref, hot_ref, hott_ref, mats_ref, mask_ref,
-    p_ref, o_ref, r_ref, kx, qx, vx,
+    lengths, live, cells, tab, tabo, qt_ref, k_ref, v_ref, cot, wo, wup, wdn, upo_in,
+    p_ref, o_ref, r_ref, hot_ref, hott_ref, dyo, woo, upo, dno,
+    kx, qx, vx, mask, mats, send, recv, *, buckets,
 ):
+    links = Links(send, recv)
+    d, m = links.d, links.m
     tokens = k_ref.shape[0]
-
-    @pl.when(pl.program_id(0) == 0)
+    rows = tokens // 2
+    width, hidden = wup.shape
+    inner = wo.shape[0]
+    step = pl.program_id(0)
+    core, cross, deep = d & 1, (d >> 1) & 1, (d >> 2) & 1
+    place = core * 4 + cross * 2 + deep
+    turned = core * 4 + deep * 2 + cross
+
+    def block(full, begin, count):
+        piece = full.shape[0] // 8
+        return full.at[rows_at(begin * piece, count * piece, piece)]
+
+    up = functools.partial(block, upo)
+    down = functools.partial(block, dno)
+    out = functools.partial(block, woo)
+    dpiece, opiece = hidden // 8, inner // 8
+    down_y = links.remote(
+        wdn.at[rows_at(turned * dpiece, dpiece, dpiece)], down(turned, 1), mp_flip=1
+    )
+    out_y = links.remote(wo.at[rows_at(place * opiece, opiece, opiece)], out(place, 1), mp_flip=1)
+    dy_y = links.remote(cot.at[1 - m], dyo, mp_flip=1)
+    up_z = links.remote(up(place, 1), up(place, 1), dp_flip=4)
+    pair = core * 4 + cross * 2
+    up_x = links.remote(up(pair, 2), up(pair, 2), dp_flip=2)
+    up_c = links.remote(up(core * 4, 4), up(core * 4, 4), dp_flip=1)
+    down_x = links.remote(down(turned, 1), down(turned, 1), dp_flip=2)
+    bent = core * 4 + deep * 2
+    down_z = links.remote(down(bent, 2), down(bent, 2), dp_flip=4)
+    down_c = links.remote(down(core * 4, 4), down(core * 4, 4), dp_flip=1)
+    out_z = links.remote(out(place, 1), out(place, 1), dp_flip=4)
+    out_x = links.remote(out(pair, 2), out(pair, 2), dp_flip=2)
+    out_c = links.remote(out(core * 4, 4), out(core * 4, 4), dp_flip=1)
+
+    def slot0():
+        links.barrier(((0, 1), (1, 0), (2, 0), (4, 0)))
+        up_z.start()
+        down_y.start()
+        out_y.start()
+        dy_y.start()
+
+    def slot4():
+        up_z.wait_recv()
+        up_x.start()
+
+    def slot5():
+        down_y.wait_recv()
+        down_x.start()
+
+    def slot6():
+        out_y.wait_recv()
+        out_z.start()
+
+    def slot9():
+        out_z.wait_recv()
+        down_x.wait_recv()
+        down_z.start()
+        out_x.start()
+
+    def slot11():
+        up_x.wait_recv()
+        up_c.start()
+
+    def last():
+        out_x.wait_recv()
+        out_c.start()
+        down_z.wait_recv()
+        down_c.start()
+        for copy in (dy_y, up_c, out_c, down_c):
+            copy.wait_recv()
+        for copy in (down_y, out_y, dy_y, up_z, up_x, up_c, down_x, down_z, down_c, out_z, out_x, out_c):
+            copy.wait_send()
+
+    slots = {0: slot0, 4: slot4, 5: slot5, 6: slot6, 9: slot9, 11: slot11}
+
+    @pl.when(step == 0)
     def _():
-        kx[:, 64:256] = hot_ref[...]
+        slot0()
         vx[64:80, :] = jnp.ones((16, tokens), BF)
+        lane = lax.broadcasted_iota(jnp.int32, (buckets, tokens), 0)
+        for t in range(3):
+            row = cells[m, t : t + 1, :]
+            hott_ref[t * buckets : (t + 1) * buckets, :] = jnp.where(row == lane, 1.0, 0.0).astype(BF)
+        hot = hott_ref[...].T
+        hot_ref[:, 0:96] = hot
+        hot_ref[:, 96:192] = hot
+        kx[:, 64:160] = hot
+        kx[:, 160:256] = hot
+        row_ids = lax.broadcasted_iota(jnp.int32, (1, tokens), 1)
+        col_ids = lax.broadcasted_iota(jnp.int32, (tokens, 1), 0)
+        seg_row = jnp.zeros((1, tokens), jnp.int32)
+        seg_col = jnp.zeros((tokens, 1), jnp.int32)
+        end = 0
+        for i in range(lengths.shape[2]):
+            end = end + lengths[m, 0, i]
+            seg_row = seg_row + jnp.where(row_ids >= end, 1, 0)
+            seg_col = seg_col + jnp.where(col_ids >= end, 1, 0)
+        live_row = live[m].astype(F32)
+        live_col = jnp.broadcast_to(live_row, (8, tokens)).T[:, 0:1]
+        code = jnp.where(live_col == 1.0, seg_col, -1)
+        allowed = (code == seg_row) | (col_ids == row_ids)
+        mask[...] = jnp.where(allowed, 0.0, MASKED)
+        line = lax.broadcasted_iota(jnp.int32, (128, 128), 0)
+        lane = lax.broadcasted_iota(jnp.int32, (128, 128), 1)
+        shift = jnp.where(lane < 64, lane, lane - 128)
+        bucket = jnp.clip(-shift, -(buckets // 2), buckets // 2 - 1) + buckets // 2
+        side = lax.broadcasted_iota(jnp.int32, (buckets, 128), 1)
+        heads = mats.shape[0] // 2
+        for part, table in enumerate((tab, tabo)):
+            exact = table[...]
+            upper = exact.astype(BF)
+            lower = (exact - upper.astype(F32)).astype(BF)
+            for t in range(3):
+                pick = jnp.where(line == bucket + t * buckets, 1.0, 0.0).astype(BF)
+                inside = (side >= t * buckets) & (side < (t + 1) * buckets)
+                for level, source in enumerate((upper, lower)):
+                    lines = dg(source, pick, 1, 0)
+                    for h in range(heads):
+                        wide = jnp.broadcast_to(lines[h : h + 1], (buckets, 128))
+                        rolled = pltpu.roll(wide, t * buckets, 1, stride=1, stride_axis=0)
+                        begin = level * 3 * buckets + t * buckets
+                        mats[part * heads + h, begin : begin + buckets, :] = jnp.where(
+                            inside, rolled, 0.0
+                        ).astype(BF)
 
     vt = v_ref[...].T
     for h in range(2):
+        for at, action in slots.items():
+            if at % 2 == h and at > 0:
+                pl.when(step == at // 2)(action)
         span = slice(64 * h, 64 * h + 64)
         kx[:, 0:64] = k_ref[:, span]
         qx[0:64, :] = qt_ref[span, :] * BF(0.125)
-        qx[64:256, :] = dg(mats_ref[h], hott_ref[...], 1, 0).astype(BF)
+        qx[64:256, :] = dg(mats[2 * step + h, :, 0:96], hott_ref[...], 1, 0).astype(BF)
         vx[0:64, :] = vt[span, :]
-        s = dg(kx[...], qx[...], 1, 0) + mask_ref[...]
+        s = dg(kx[...], qx[...], 1, 0) + mask[...]
         top = jnp.max(s, axis=0, keepdims=True)
         p = jnp.exp(s - top).astype(BF)
         p_ref[h] = p
@@ -237,43 +325,62 @@
         r = 1.0 / o[64:65, :]
         o_ref[span, :] = (o[0:64] * r).astype(BF)
         r_ref[0, h : h + 1, :] = r
-
-
-def attend(qt, kv, hot, hott, mats, mask):
+    pl.when(step == pl.num_programs(0) - 1)(last)
+
+
+def attend(lengths, live, cells, tab, tabo, qt, kv, cot, wo, wup, wdn, upo, buckets):
     channels, tokens = qt.shape
+    width, hidden = wup.shape
+    inner = wo.shape[0]
     pairs = channels // 128
     half = pairs // 2
     whole = lambda shape: pl.BlockSpec(shape, lambda i: (0,) * len(shape))
     return pl.pallas_call(
-        attend_kernel,
+        functools.partial(attend_kernel, buckets=buckets),
         grid=(pairs,),
         in_specs=[
+            pl.BlockSpec(memory_space=pltpu.SMEM),
+            whole(live.shape),
+            whole(cells.shape),
+            whole(tab.shape),
+            whole(tabo.shape),
             pl.BlockSpec((128, tokens), lambda i: (i, 0)),
             pl.BlockSpec((tokens, 128), lambda i: (0, (i // half) * 2 * half + i % half)),
             pl.BlockSpec((tokens, 128), lambda i: (0, (i // half) * 2 * half + half + i % half)),
-            whole((tokens, 192)),
-            whole((96, tokens)),
-            pl.BlockSpec((2, 192, 96), lambda i: (i, 0, 0)),
-            whole((tokens, tokens)),
+            ANY, ANY, ANY, ANY, ANY,
         ],
         out_specs=[
             pl.BlockSpec((2, tokens, tokens), lambda i: (i, 0, 0)),
             pl.BlockSpec((128, tokens), lambda i: (i, 0)),
             pl.BlockSpec((1, 2, tokens), lambda i: (i, 0, 0)),
+            whole((tokens, 192)),
+            whole((96, tokens)),
+            ANY, ANY, ANY, ANY,
         ],
         out_shape=[
             SHAPE((2 * pairs, tokens, tokens), BF),
             SHAPE((channels, tokens), BF),
             SHAPE((pairs, 2, tokens), F32),
-        ],
+            SHAPE((tokens, 192), BF),
+            SHAPE((96, tokens), BF),
+            SHAPE((tokens // 2, width), BF),
+            SHAPE((inner, width), BF),
+            SHAPE((width, hidden), BF),
+            SHAPE((hidden, width), BF),
+        ],
+        input_output_aliases={12: 7},
         scratch_shapes=[
             pltpu.VMEM((tokens, 256), BF),
             pltpu.VMEM((256, tokens), BF),
             pltpu.VMEM((80, tokens), BF),
-        ],
-        compiler_params=params(),
+            pltpu.VMEM((tokens, tokens), F32),
+            pltpu.VMEM((2 * pairs, 192, 128), BF),
+            pltpu.SemaphoreType.DMA((20,)),
+            pltpu.SemaphoreType.DMA((20,)),
+        ],
+        compiler_params=params(58, collective_id=3, has_side_effects=True),
         name="attend",
-    )(qt, kv, kv, hot, hott, mats, mask)
+    )(lengths, live, cells, tab, tabo, qt, kv, kv, cot, wo, wup, wdn, upo)
 
 
 def attend_back_kernel(
@@ -347,14 +454,22 @@
 
 
 def middle_kernel(
-    x_ref, mixt_ref, wo_ref, dy_ref, gain_ref, wup_ref, wdn_ref,
+    x_ref, mixt_ref, wo_in, woo_in, cot, dyo, gain_ref, wup_in, upo_in, wdn_in, dno_in,
     y_ref, gup_ref, gdn_ref, gwo_ref, dh_ref, dmt_ref, gg_ref,
-    h1, n2, n2t, yacc, dn,
+    h1, n2, n2t, yacc, dn, wo_ref, dy_ref,
 ):
     step = pl.program_id(0)
+    early = step < pl.num_programs(0) // 2
 
     @pl.when(step == 0)
     def _():
+        m = lax.axis_index("mp")
+        rows = dyo.shape[0]
+        dy_ref[rows_at(m * rows, rows, rows)] = cot[m]
+        dy_ref[rows_at((1 - m) * rows, rows, rows)] = dyo[...]
+        inner = wo_in.shape[0]
+        wo_ref[0:inner] = wo_in[...]
+        wo_ref[inner:] = woo_in[...]
         added = dg(mixt_ref[...], wo_ref[...], 0, 0)
         h = x_ref[...].astype(F32) + added
         h1[...] = h
@@ -365,7 +480,9 @@
         n2t[...] = normed.T
         dn[...] = jnp.zeros_like(dn)
 
-    wup, wdn, dy = wup_ref[...], wdn_ref[...], dy_ref[...]
+    wup = jnp.where(early, upo_in[...], wup_in[...])
+    wdn = jnp.where(early, dno_in[...], wdn_in[...])
+    dy = dy_ref[...]
     u = dg(n2[...], wup, 1, 0)
     cdf = 0.5 * (1.0 + lax.erf(u * 0.7071067811865476))
     act = (u * cdf).astype(BF)
@@ -393,26 +510,34 @@
         dmt_ref[...] = dg(wo_ref[...], low, 1, 1).astype(BF)
 
 
-def middle(x, mixt, wo, dy, gain, wup, wdn, chunk=512):
+def middle(x, mixt, wo, woo, cot, dyo, gain, wup, upo, wdn, dno, chunk=512):
     tokens, width = x.shape
-    hidden = wup.shape[1]
+    hidden = 2 * wup.shape[1]
+    n = hidden // chunk
     whole = lambda shape: pl.BlockSpec(shape, lambda i: (0,) * len(shape))
+    late = lambda i: jnp.maximum(i - n // 2, 0)
+    early = lambda i: jnp.minimum(i, n // 2 - 1)
+    slot = lambda i: lax.rem(i + n // 2, n)
     return pl.pallas_call(
         middle_kernel,
-        grid=(hidden // chunk,),
+        grid=(n,),
         in_specs=[
             whole((tokens, width)),
             whole((width, tokens)),
-            whole((width, width)),
-            whole((tokens, width)),
+            whole(wo.shape),
+            whole(woo.shape),
+            whole(cot.shape),
+            whole(dyo.shape),
             whole((1, width)),
-            pl.BlockSpec((width, chunk), lambda i: (0, i)),
-            pl.BlockSpec((chunk, width), lambda i: (i, 0)),
+            pl.BlockSpec((width, chunk), lambda i: (0, late(i))),
+            pl.BlockSpec((width, chunk), lambda i: (0, early(i))),
+            pl.BlockSpec((chunk, width), lambda i: (late(i), 0)),
+            pl.BlockSpec((chunk, width), lambda i: (early(i), 0)),
         ],
         out_specs=[
             whole((tokens, width)),
-            pl.BlockSpec((width, chunk), lambda i: (0, i)),
-            pl.BlockSpec((chunk, width), lambda i: (i, 0)),
+            pl.BlockSpec((width, chunk), lambda i: (0, slot(i))),
+            pl.BlockSpec((chunk, width), lambda i: (slot(i), 0)),
             whole((width, width)),
             whole((tokens, width)),
             whole((width, tokens)),
@@ -433,10 +558,12 @@
             pltpu.VMEM((width, tokens), BF),
             pltpu.VMEM((tokens, width), F32),
             pltpu.VMEM((tokens, width), F32),
+            pltpu.VMEM((width, width), BF),
+            pltpu.VMEM((tokens, width), BF),
         ],
         compiler_params=params(60),
         name="middle",
-    )(x, mixt, wo, dy, gain, wup, wdn)
+    )(x, mixt, wo, woo, cot, dyo, gain, wup, upo, wdn, dno)
 
 
 def finish_kernel(
@@ -695,49 +822,24 @@
     heads = third // HDIM
     buckets = tables.shape[1]
     half = buckets // 2
-    m = lax.axis_index("mp")
-
-    resid = inputs.astype(F32) + roi.astype(F32)
     tab = jnp.pad(
         tables.transpose(2, 0, 1).reshape(heads, 3 * buckets), ((0, 2), (0, 128 - 3 * buckets))
     )
-    x, dy, tab_other, wqkv, wo, wup, wdn = gather(
-        resid.astype(BF), cotangent, tab, w_query, w_key, w_value, w_out, w_up, w_down
+    ga, gf = gain_attn.reshape(1, width), gain_ffn.reshape(1, width)
+    x, tabo, wqkv, qt, kv, upo = entry(
+        inputs, roi, tab, ga, w_query, w_key, w_value, w_up
     )
-
-    lengths = lax.dynamic_index_in_dim(doc_lengths, m, 0, keepdims=False)[0]
-    live = lax.dynamic_index_in_dim(live_mask, m, 0, keepdims=False)
-    cells = lax.dynamic_index_in_dim(bucket_cells, m, 0, keepdims=False)
-    ids = jnp.arange(tokens)
-    segment = jnp.sum((ids[:, None] >= jnp.cumsum(lengths)[None, :]).astype(jnp.int32), axis=1)
-    allowed = (segment[:, None] == segment[None, :]) & (
-        (live[:, None] == 1) | (ids[:, None] == ids[None, :])
+    p, mixt, r, hot, hott, dyo, woo, upo, dno = attend(
+        doc_lengths, live_mask.reshape(2, 1, tokens), bucket_cells, tab, tabo, qt, kv,
+        cotangent, w_out, w_up, w_down, upo, buckets,
     )
-    mask = jnp.where(allowed, 0.0, MASKED).astype(F32)
+    y, gup, gdn, gwo, dh, dmt, gain_f = middle(x, mixt, w_out, woo, cotangent, dyo, gf, w_up, upo, w_down, dno)
+    dq, dk, dv, gmats = attend_back(p, qt, kv, mixt, dmt, r, hott, hot)
+    gqkv, gin, gain_a = finish(x, ga, dh, dq, dk, dv, wqkv)
+
     cell_ids = jnp.arange(buckets)
-    hott = (cells[:, None, :] == cell_ids[None, :, None]).astype(BF).reshape(3 * buckets, tokens)
-    hot = (cells.T[:, :, None] == cell_ids[None, None, :]).astype(BF).reshape(tokens, 3 * buckets)
-    hot = jnp.concatenate([hot, hot], axis=1)
     relative = jnp.clip(cell_ids[:, None] - cell_ids[None, :], -half, half - 1) + half
     select = (relative[:, :, None] == cell_ids).astype(F32)
-    both = jnp.concatenate([tab[:heads], tab_other[:heads]], 0)[:, : 3 * buckets]
-    both = both.reshape(2 * heads, 3, buckets)
-    blocks = jnp.einsum("han,xyn->haxy", both, select, precision=lax.Precision.HIGHEST)
-    eye = jnp.eye(3, dtype=F32)
-    mats = (blocks[:, :, :, None, :] * eye[None, :, None, :, None]).reshape(
-        2 * heads, 3 * buckets, 3 * buckets
-    )
-    mats_hi = mats.astype(BF)
-    mats_lo = (mats - mats_hi.astype(F32)).astype(BF)
-    mats = jnp.concatenate([mats_hi, mats_lo], axis=1)
-
-    ga, gf = gain_attn.reshape(1, width), gain_ffn.reshape(1, width)
-    qt, kv = project(x, ga, wqkv)
-    p, mixt, r = attend(qt, kv, hot, hott, mats, mask)
-    y, gup, gdn, gwo, dh, dmt, gain_f = middle(x, mixt, wo, dy, gf, wup, wdn)
-    dq, dk, dv, gmats = attend_back(p, qt, kv, mixt, dmt, r, hott, hot)
-    gqkv, gin, gain_a = finish(x, ga, dh, dq, dk, dv, wqkv)
-
     gblocks = jnp.stack(
         [gmats[:, t * buckets : (t + 1) * buckets, t * buckets : (t + 1) * buckets] for t in range(3)],
         axis=1,
@@ -751,7 +853,7 @@
     )
     yret, gret, small, fqkv, fwo, fup, fdn = reduce_all(y, gin, small, gqkv, gwo, gup, gdn, n_dp)
     lines = width // 128
-    out = resid + yret.astype(F32)
+    out = inputs.astype(F32) + roi.astype(F32) + yret.astype(F32)
     grad_in = cotangent.astype(F32) + gret.astype(F32)
     table_out = small[16 : 16 + heads, : 3 * buckets].reshape(heads, 3, buckets).transpose(1, 2, 0)
     return (

time: 448 us -> 391 us (0.87)
  Pallas kernels: 383 us -> 355 us
  local copies, waits for them, and re-layouts: 28.2 us -> 10 us
  other arithmetic: 25.7 us -> 16.8 us
    pallas_call x4 -> x3, Pallas kernels: 166 us -> 138 us  [the longest x1 53.2 us: attend(): pl.pallas_call(functools.partial(attend_kernel, buckets=buckets), grid=(p...]
    unnamed x50 -> x20, local copies, waits for them, and re-layouts: 18 us -> 3.44 us
    mul x4 -> x0, local copies, waits for them, and re-layouts: 4.88 us -> none  [local(): blocks[:, :, :, None, :] * eye[None, :, None, :, None]]
where the time goes in v2:
time: 391 us; the launch traced here: 384 us
  Pallas kernels  355 us (91%)
  other arithmetic  16.8 us (4%)
  local copies, waits for them, and re-layouts  10 us (3%)
    pallas_call x1, Pallas kernels, reduce_all(): pl.pallas_call(functools.partial(reduce_kernel, n_dp=n_dp), out_shape=[SH...  166 us
    pallas_call x1, Pallas kernels, attend(): pl.pallas_call(functools.partial(attend_kernel, buckets=buckets), grid=(p...  53.2 us
    pallas_call x1, Pallas kernels, middle(): pl.pallas_call(middle_kernel, grid=(n,), in_specs=[whole((tokens, width))...  45.7 us
    pallas_call x1, Pallas kernels, entry(): pl.pallas_call(entry_kernel, out_shape=[SHAPE((tokens, width), BF), SHAPE...  39.5 us
    pallas_call x1, Pallas kernels, attend_back(): pl.pallas_call(attend_back_kernel, grid=(pairs,), in_specs=[pl.BlockSpec(...  32.1 us
    pallas_call x1, Pallas kernels, finish(): pl.pallas_call(functools.partial(finish_kernel, third=third), grid=(2,),...  18.6 us

profile of v2, /device:TPU:0, one launch (start us, length us, event | category | flops | bytes accessed | tf_op | source)
XLA Modules:
  0.0 383.6 jit_solution(6217762795443152046)
XLA Ops:
  0.6 0.7 copy.32
  1.4 0.1 reshape.69
  1.4 0.6 pad.8.tab
  2.0 1.3 reshape.70.gain.gain_ref
  3.3 0.0 copy-start.4
  3.3 0.0 copy-start.6
  3.3 39.5 %entry.1 = (bf16[1024,768]{1,0:T(8,128)(2,1)}, f32[8,128]{1,0:T(8,128)}, bf16[768,2304]{1,0:T(8,128)(2,1)}, bf16[768,1024]{1,0:T(8,128)(2,1)}, bf16[1024,1536]{1,0:T(8,128)(2,1)}, /*index=5*/bf16[768,1536]{1,0:T(8,128)(2,1)}) custom-call(bf16[2,512,768]{2,1,0:T(8,128)(2,1)} %inp.1, bf16[2,512,768]{2,1,0:T(8,128)(2,1)} %roi.1, f32[8,128]{1,0:T(8,128)} %pad.8.tab, ...), custom_call_target="tpu_custom_call" | custom-call | tf_op jit(solution)/shard_map/entry/pallas_call | solution.py:155
  42.8 0.0 copy-done.4
  42.8 0.6 copy.33.cells
  43.4 0.0 copy-done.6
  43.4 0.6 reshape.71.live
  44.0 0.0 copy-start.7
  44.0 53.2 %attend.1 = (bf16[12,1024,1024]{2,1,0:T(8,128)(2,1)}, bf16[768,1024]{1,0:T(8,128)(2,1)}, f32[6,2,1024]{2,1,0:T(2,128)}, bf16[1024,192]{1,0:T(8,128)(2,1)}, bf16[...) custom-call(s32[2,1,8]{2,1,0:T(1,128)} %lengths.1, ...), custom_call_target="tpu_custom_call", output_to_operand_aliasing={{7}: (12, {})} | custom-call | tf_op jit(solution)/shard_map/attend/pallas_call | solution.py:338
  97.3 0.0 copy-done.7
  97.3 0.6 reshape.72.gain_ref
  97.8 45.7 %middle.1 = (bf16[1024,768]{1,0:T(8,128)(2,1)}, bf16[768,3072]{1,0:T(8,128)(2,1)}, bf16[3072,768]{1,0:T(8,128)(2,1)}, bf16[768,768]{1,0:T(8,128)(2,1)}, f32[1024...) custom-call(bf16[1024,768]{1,0:T(8,128)(2,1)} %get-tuple-element.47.x_ref, ...), custom_call_target="tpu_custom_call" | custom-call | tf_op jit(solution)/shard_map/middle/pallas_call | solution.py:521
  143.6 32.1 %attend_back.1 = (bf16[1024,768]{1,0:T(8,128)(2,1)}, bf16[1024,768]{1,0:T(8,128)(2,1)}, bf16[1024,768]{1,0:T(8,128)(2,1)}, f32[12,96,96]{2,1,0:T(8,128)}) custom-call(bf16[12,1024,1024]{2,1,0:T(8,128)(2,1)} %get-tuple-element.59.p_ref, bf16[768,1024]{1,0:T(8,128)(2,1)} %get-tuple-element.49.qt_ref, bf16[1024,1536]{1,0:T(8,128)(2,1)} %get-tuple-element.50.k_ref.v_ref, ...), custom_call_target="tpu_custom_call" | custom-call | tf_op jit(solution)/shard_map/attend_back/pallas_call | solution.py:430
  175.6 1.3 slice_bitcast_fusion.2
  176.9 0.1 pad_maximum_fusion
  177.0 0.8 convolution_bitcast_fusion
  177.8 0.1 reshape.75
  177.9 0.0 copy-start.8
  177.9 18.6 %finish.1 = (bf16[768,2304]{1,0:T(8,128)(2,1)}, bf16[1024,768]{1,0:T(8,128)(2,1)}, f32[1,768]{1,0:T(1,128)}) custom-call(bf16[1024,768]{1,0:T(8,128)(2,1)} %get-tuple-element.47.x_ref, f32[1,768]{1,0:T(1,128)} %reshape.70.gain.gain_ref, f32[1024,768]{1,0:T(8,128)} %get-tuple-element.58.dh_ref, bf16[1024,768]{1,0:T(8,128)(2,1)} %get-tuple-element.64.dq_ref, ...), custom_call_target="tpu_custom_call" | custom-call | tf_op jit(solution)/shard_map/finish/pallas_call | solution.py:605
  196.5 0.7 reduce.1
  197.2 0.0 copy-done.8
  197.3 0.1 pad.12.clone
  197.3 0.7 pad_maximum_fusion.1.small
  198.0 165.6 %reduce.3 = (bf16[2,512,768]{2,1,0:T(8,128)(2,1)}, bf16[2,512,768]{2,1,0:T(8,128)(2,1)}, f32[32,128]{1,0:T(8,128)}, bf16[768,1152]{1,0:T(8,128)(2,1)}, bf16[768,...) custom-call(bf16[1024,768]{1,0:T(8,128)(2,1)} %get-tuple-element.57.y, ...), custom_call_target="tpu_custom_call" | custom-call | tf_op jit(solution)/shard_map/reduce/pallas_call | solution.py:799
  363.6 0.0 copy-start.1
  363.7 4.0 %slice_convert_fusion = (f32[768,384]{1,0:T(8,128)}, f32[768,384]{1,0:T(8,128)}, f32[768,384]{1,0:T(8,128)}, f32[384,768]{0,1:T(8,128)}) fusion(bf16[768,1152]{1,0:T(8,128)(2,1)} %get-tuple-element.79, bf16[768,384]{1,0:T(8,128)(2,1)} %get-tuple-element.80), kind=kLoop, calls=%fused_computation.6 | loop fusion | flops 1179648 | bytes 7077888 | tf_op jit(solution)/shard_map/convert_element_type | solution.py:866
  367.6 0.0 copy-start
  367.7 2.8 copy.37
  370.4 0.0 copy-done.1
  370.4 0.0 copy-done
  370.4 0.0 copy-start.3
  370.4 6.0 %convert_add_fusion = (f32[2,512,768]{2,1,0:T(8,128)}, f32[2,512,768]{2,1,0:T(8,128)}) fusion(bf16[2,512,768]{2,1,0:T(8,128)(2,1)} %get-tuple-element.77, bf16[2,512,768]{2,1,0:T(8,128)(2,1)S(1)} %copy-done, bf16[2,512,768]{2,1,0:T(8,128)(2,1)} %get-tuple-element.76, bf16[2,512,768]{2,1,0:T(8,128)(2,1)} %roi.1, bf16[2,512,768]{2,1,0:T(8,128)(2,1)S(1)} %copy-done.1), kind=kLoop, calls=%fused_computation | loop fusion | flops 6291456 | bytes 14155776 | tf_op jit(solution)/shard_map/add | solution.py:857
  376.4 0.0 copy-done.3
  376.4 0.0 copy-start.2
  376.4 2.8 convert_element_type.51
  379.3 0.0 copy-done.2
  379.3 0.0 copy-start.5
  379.3 2.5 convert_element_type.52
  381.8 0.0 copy-done.5
  381.8 0.1 reshape.79
  381.9 0.6 copy.42
  382.5 0.6 slice_bitcast_fusion.3
  (6 shorter events, 0.0 us)
Async XLA Ops:
  3.3 39.5 %copy-start.4 = (s32[2,3,1024]{2,0,1:T(2,128)S(1)}, s32[2,3,1024]{2,0,1:T(2,128)}, u32[]{:S(2)}) copy-start(s32[2,3,1024]{2,0,1:T(2,128)} %param.20) | copy-start | bytes 73732
  3.3 40.1 %copy-start.6 = (s32[2,1024]{1,0:T(2,128)S(1)}, s32[2,1024]{1,0:T(2,128)}, u32[]{:S(2)}) copy-start(s32[2,1024]{1,0:T(2,128)} %param.19) | copy-start | bytes 24580
  44.0 53.2 %copy-start.7 = (f32[768]{0:T(1024)S(1)}, f32[768]{0:T(1024)}, u32[]{:S(2)}) copy-start(f32[768]{0:T(1024)} %param.22) | copy-start | bytes 9220
  177.9 19.3 %copy-start.8 = (f32[1,768]{1,0:T(1,128)S(1)}, f32[1,768]{1,0:T(1,128)}, u32[]{:S(2)}) copy-start(f32[1,768]{1,0:T(1,128)} %get-tuple-element.70) | copy-start | bytes 9220
  363.6 6.8 %copy-start.1 = (bf16[2,512,768]{2,1,0:T(8,128)(2,1)S(1)}, bf16[2,512,768]{2,1,0:T(8,128)(2,1)}, u32[]{:S(2)}) copy-start(bf16[2,512,768]{2,1,0:T(8,128)(2,1)} %inp.1) | copy-start | bytes 4718596
  367.6 2.8 copy-start
  370.4 6.0 %copy-start.3 = (bf16[768,1536]{1,0:T(8,128)(2,1)S(1)}, bf16[768,1536]{1,0:T(8,128)(2,1)}, u32[]{:S(2)}) copy-start(bf16[768,1536]{1,0:T(8,128)(2,1)} %get-tuple-element.81) | copy-start | bytes 7077892
  376.4 2.8 copy-start.2
  379.3 2.5 copy-start.5
